TPU v7x, 256 devices: a whole 4x4x8 slice. The times are simulated.
256 devices in a mesh: context: 64 (over y, x_lo, z), heads: 4 (over x_hi, core).
Axes of the slice: x: 4 (x_hi: 2, x_lo: 2; x = x_hi * 2 + x_lo), y: 4, z: 8, core: 2. Of those that a mesh axis runs over, the one named last changes fastest.
Arguments:
- upstream: bfloat16 [16384, 1024], P(('context', 'heads')), may hold values from -48 to 48
- out_weight: bfloat16 [1024, 1024], P('heads'), may hold values from -0.1875 to 0.1875
- query_rows: bfloat16 [16384, 1024], P('context', 'heads'), may hold values from -6 to 6
- key_rows: bfloat16 [16384, 1024], P('context', 'heads'), may hold values from -6 to 6
- value_rows: bfloat16 [16384, 1024], P('context', 'heads'), may hold values from -6 to 6
- head_offsets: int32 [16], replicated, may hold values from 0 to 15, each once
Outputs:
- query_grad: bfloat16 [16384, 1024], P('context', 'heads')
- key_grad: bfloat16 [16384, 1024], P('context', 'heads')
- value_grad: bfloat16 [16384, 1024], P('context', 'heads')
Inputs may be any that keep to these rules, and one draw needn't show every extreme that they name: `head_offsets`: every value of 0 to 15 occurs once.
All inputs are finite; a program needn't handle non-finite values.
Results may differ from a plain program's by a relative error of at most 0.008.
Values may be sent and summed in bfloat16 or wider, within the bound.
A program may use at most 128 MiB of HBM per device.

v0:
```python
import math

import jax
import jax.numpy as jnp
from jax import lax
from jax.sharding import PartitionSpec as P

HEAD_SIZE = 64
DILATION_RATE = 16
FIRST_SEGMENT = 2048


def partner_2(value, axis, apart):
    mask = 2**apart
    pairs = [(source, source ^ mask) for source in range(lax.axis_size(axis))]
    return lax.ppermute(value, axis, pairs)


def dot_rows(left, right):
    return lax.dot_general(
        left, right, (((1,), (1,)), ((), ())), preferred_element_type=jnp.float32
    )


def dot_cols(left, right):
    return lax.dot_general(
        left, right, (((0,), (0,)), ((), ())), preferred_element_type=jnp.float32
    )


def pick_rows(payload_arrays, mask_stack):
    span_length, block_width = payload_arrays.shape
    head_count = mask_stack.shape[1]
    launch_layout = payload_arrays.reshape(
        span_length // DILATION_RATE, DILATION_RATE, head_count, block_width // head_count
    )
    selected_rows = jnp.where(
        mask_stack[None, :, :, None], launch_layout, jnp.zeros((), payload_arrays.dtype)
    )
    return jnp.sum(selected_rows, axis=1).reshape(span_length // DILATION_RATE, block_width)


def place_rows(picked, mask_stack):
    total_count, block_width = picked.shape
    head_count = mask_stack.shape[1]
    launch_layout = picked.reshape(total_count, 1, head_count, block_width // head_count)
    dispersal_rows = jnp.where(
        mask_stack[None, :, :, None], launch_layout, jnp.zeros((), picked.dtype)
    )
    return dispersal_rows.reshape(total_count * DILATION_RATE, block_width)


def spread_rows(value_tensor, head_shift):
    total_count = value_tensor.shape[0]
    matched_flag = jnp.arange(DILATION_RATE, dtype=jnp.int32)[None, :] == head_shift
    return jnp.where(
        matched_flag, value_tensor[:, None], jnp.zeros((), value_tensor.dtype)
    ).reshape(total_count * DILATION_RATE)


def double_up(buffer, levels, position):
    for level in range(levels):
        partner = partner_2(buffer, "context", level)
        lower = position >> level & 1 == 0
        buffer = jnp.where(
            lower, jnp.concatenate([buffer, partner], 1), jnp.concatenate([partner, buffer], 1)
        )
    return buffer


def halve_down(buffer, levels, position):
    for level in range(levels - 1, -1, -1):
        middle = buffer.shape[1] // 2
        lower_half = buffer[:, :middle]
        upper_half = buffer[:, middle:]
        lower = position >> level & 1 == 0
        kept = jnp.where(lower, lower_half, upper_half)
        outgoing = jnp.where(lower, upper_half, lower_half)
        incoming = partner_2(outgoing, "context", level)
        buffer = kept + incoming
    return buffer


def body(upstream, out_weight, query_rows, key_rows, value_rows, head_offsets):
    position = lax.axis_index("context")
    span_length, block_width = query_rows.shape
    head_count = block_width // HEAD_SIZE
    scale = 1.0 / math.sqrt(HEAD_SIZE)
    partial_rows = dot_rows(upstream, lax.all_gather(out_weight, "heads", axis=0, tiled=True))
    attn_grad = lax.all_to_all(
        partial_rows.astype(jnp.bfloat16), "heads", split_axis=1, concat_axis=0, tiled=True
    )
    local_shifts = lax.dynamic_slice_in_dim(
        head_offsets, lax.axis_index("heads") * head_count, head_count
    )
    mask_stack = jnp.arange(DILATION_RATE, dtype=jnp.int32)[:, None] == local_shifts[None, :]
    query_pick = pick_rows(query_rows, mask_stack)
    grad_pick = pick_rows(attn_grad, mask_stack)
    key_pick = pick_rows(key_rows, mask_stack)
    value_pick = pick_rows(value_rows, mask_stack)
    picked_pair = jnp.stack([key_pick, value_pick])
    dense_span = FIRST_SEGMENT // span_length
    dense_levels = dense_span.bit_length() - 1
    near_pair = double_up(jnp.stack([key_rows, value_rows]), dense_levels, position)
    far_pair = lax.all_gather(picked_pair, "context", axis=1, tiled=True)
    block_rows = min(512, span_length)
    num_blocks = span_length // block_rows
    current_row_index = jnp.arange(span_length, dtype=jnp.int32)
    dq_near_list, dk_near_list, dv_near_list = ([], [], [])
    dq_far_list, dk_far_list, dv_far_list = ([], [], [])
    lse_list, delta_list = ([], [])
    for head in range(head_count):
        columns = slice(head * HEAD_SIZE, (head + 1) * HEAD_SIZE)
        head_shift = local_shifts[head]
        query_head = query_rows[:, columns]
        grad_head = attn_grad[:, columns]
        near_keys = near_pair[0][:, columns]
        near_values = near_pair[1][:, columns]
        query_sel = query_pick[:, columns]
        grad_sel = grad_pick[:, columns]
        far_keys = far_pair[0][:, columns]
        far_values = far_pair[1][:, columns]
        score_near = dot_rows(query_sel, near_keys) * scale
        score_far = dot_rows(query_sel, far_keys) * scale
        row_max = jnp.maximum(jnp.max(score_near, 1), jnp.max(score_far, 1))
        row_sum = jnp.sum(jnp.exp(score_near - row_max[:, None]), 1) + jnp.sum(
            jnp.exp(score_far - row_max[:, None]), 1
        )
        lse_sel = row_max + jnp.log(row_sum)
        prob_near = jnp.exp(score_near - lse_sel[:, None])
        prob_far = jnp.exp(score_far - lse_sel[:, None])
        dprob_near = dot_rows(grad_sel, near_values)
        dprob_far = dot_rows(grad_sel, far_values)
        delta_sel = jnp.sum(prob_near * dprob_near, 1) + jnp.sum(prob_far * dprob_far, 1)
        dscore_far = (prob_far * (dprob_far - delta_sel[:, None])).astype(jnp.bfloat16)
        dq_far_list.append(
            jnp.dot(dscore_far, far_keys, preferred_element_type=jnp.float32) * scale
        )
        lse_list.append(lse_sel)
        delta_list.append(delta_sel)
        prob_far16 = prob_far.astype(jnp.bfloat16)
        dk_far_list.append(dot_cols(dscore_far, query_sel) * scale)
        dv_far_list.append(dot_cols(prob_far16, grad_sel))
        lse_rows = spread_rows(lse_sel, head_shift)
        delta_rows = spread_rows(delta_sel, head_shift)
        selected_rows = current_row_index % DILATION_RATE == head_shift

        def step(carry, inputs):
            key_acc, value_acc = carry
            query_blk, grad_blk, lse_blk, delta_blk, mask_blk = inputs
            scores = dot_rows(query_blk, near_keys) * scale
            blk_max = jnp.max(scores, 1)
            blk_sum = jnp.sum(jnp.exp(scores - blk_max[:, None]), 1)
            lse_all = jnp.where(mask_blk, lse_blk, blk_max + jnp.log(blk_sum))
            probs = jnp.exp(scores - lse_all[:, None])
            dprobs = dot_rows(grad_blk, near_values)
            delta_all = jnp.where(mask_blk, delta_blk, jnp.sum(probs * dprobs, 1))
            dscores = (probs * (dprobs - delta_all[:, None])).astype(jnp.bfloat16)
            probs16 = probs.astype(jnp.bfloat16)
            dq_blk = jnp.dot(dscores, near_keys, preferred_element_type=jnp.float32) * scale
            key_acc = key_acc + dot_cols(dscores, query_blk) * scale
            value_acc = value_acc + dot_cols(probs16, grad_blk)
            return ((key_acc, value_acc), dq_blk)

        zeros_acc = jnp.zeros((near_keys.shape[0], HEAD_SIZE), jnp.float32)
        (key_acc, value_acc), dq_blocks = lax.scan(
            step,
            (zeros_acc, zeros_acc),
            (
                query_head.reshape(num_blocks, block_rows, HEAD_SIZE),
                grad_head.reshape(num_blocks, block_rows, HEAD_SIZE),
                lse_rows.reshape(num_blocks, block_rows),
                delta_rows.reshape(num_blocks, block_rows),
                selected_rows.reshape(num_blocks, block_rows),
            ),
        )
        dq_near_list.append(dq_blocks.reshape(span_length, HEAD_SIZE))
        dk_near_list.append(key_acc)
        dv_near_list.append(value_acc)
    near_terms = jnp.stack([jnp.concatenate(dk_near_list, 1), jnp.concatenate(dv_near_list, 1)])
    near_back = halve_down(near_terms, dense_levels, position)
    far_terms = jnp.stack([jnp.concatenate(dk_far_list, 1), jnp.concatenate(dv_far_list, 1)])
    far_back = lax.psum_scatter(far_terms, "context", scatter_dimension=1, tiled=True)
    far_key_grad = far_back[0]
    far_value_grad = far_back[1]
    query_grad = (
        jnp.concatenate(dq_near_list, 1) + place_rows(jnp.concatenate(dq_far_list, 1), mask_stack)
    ).astype(jnp.bfloat16)
    key_grad = (near_back[0] + place_rows(far_key_grad, mask_stack)).astype(jnp.bfloat16)
    value_grad = (near_back[1] + place_rows(far_value_grad, mask_stack)).astype(jnp.bfloat16)
    return (query_grad, key_grad, value_grad)


def solution(mesh):
    return jax.shard_map(
        body,
        mesh=mesh,
        in_specs=(
            P(("context", "heads"), None),
            P("heads", None),
            P("context", "heads"),
            P("context", "heads"),
            P("context", "heads"),
            P(),
        ),
        out_specs=(P("context", "heads"), P("context", "heads"), P("context", "heads")),
        check_vma=False,
    )
```

profile of v0, /device:TPU:4, one launch (start us, length us, event | category | flops | bytes accessed | tf_op | source)
XLA Modules:
  0.0 1150.2 jit_solution(13889192455797140097)
XLA Ops:
  8.3 2.0 collective-permute-start
  10.4 6.2 collective-permute-done
  16.6 1.3 maximum_select_fusion.2
  17.9 3.4 collective-permute-start.1
  21.2 22.5 %collective-permute-done.1 = bf16[2,512,256]{2,1,0:T(8,128)(2,1)S(1)} collective-permute-done((bf16[2,512,256]{2,1,0:T(8,128)(2,1)S(1)}, bf16[2,512,256]{2,1,0:T(8,128)(2,1)S(1)}, u32[]{:S(2)}, u32[]{:S(2)}) %collective-permute-start.1) | collective-permute-done | bytes 524320 | tf_op jit(solution)/shard_map/ppermute | solution.py:16
  44.0 6.3 collective-permute-start.2
  54.9 1.2 iota_compare_fusion.4
  56.0 1.1 iota_compare_fusion.1
  58.2 1.2 iota_compare_fusion.3
  59.5 36.6 %collective-permute-done.2 = bf16[2,1024,256]{2,1,0:T(8,128)(2,1)S(1)} collective-permute-done((bf16[2,1024,256]{2,1,0:T(8,128)(2,1)S(1)}, bf16[2,1024,256]{2,1,0:T(8,128)(2,1)S(1)}, u32[]{:S(2)}, u32[]{:S(2)}) %collective-permute-start.2) | collective-permute-done | bytes 1048608 | tf_op jit(solution)/shard_map/ppermute | solution.py:16
  96.5 1.2 slice_bitcast_fusion.1
  97.7 1.9 fusion.135
  100.2 2.3 convolution_convert_fusion
  103.2 4.8 all-to-all-start
  108.0 2.5 exponential_reduce_fusion
  111.8 2.0 select_reduce_fusion.3
  116.4 1.3 copy-done.6
  119.2 1.3 copy-done.3
  121.6 1.6 fusion.133
  123.2 1.6 fusion.131
  124.8 1.6 fusion.129
  126.4 1.6 fusion.127
  128.0 284.4 %all-gather.3.cloned.1.call-done = bf16[2,1024,256]{2,1,0:T(8,128)(2,1)} async-done(((bf16[2,16,256]{2,1,0:T(8,128)(2,1)}), bf16[2,1024,256]{2,1,0:T(8,128)(2,1)}) %all-gather.3.cloned.1.call-update) | async-done | bytes 1048592 | tf_op jit(solution)/shard_map/all_gather | solution.py:105
  412.4 1.4 slice_bitcast_fusion.3
  417.2 1.8 fusion.9
  419.0 1.4 multiply_reduce_fusion.3
  421.9 1.6 multiply_reduce_fusion.2
  424.9 1.5 multiply_reduce_fusion.1
  430.0 1.3 select_n.327
  431.3 1.5 add_select_fusion
  432.8 2.9 fusion.16
  435.7 3.5 fusion.1
  440.0 1.3 select_n.321
  441.3 1.3 add_select_fusion.1
  442.5 1.3 fusion.15
  443.8 2.4 fusion.3
  447.0 1.4 select_n.315
  448.4 1.5 add_select_fusion.2
  449.8 2.9 fusion.14
  452.8 3.6 fusion.5
  457.1 1.4 select_n.308
  458.4 1.5 add_select_fusion.3
  459.9 2.8 fusion.13
  462.8 3.5 fusion.7
  466.4 1.3 select_n.312
  468.7 1.3 select_n.318
  470.9 1.4 select_n.324
  473.3 1.4 select_n.330
  475.5 1.3 fusion.125
  476.8 2.8 fusion.2
  481.8 1.2 fusion.123
  484.4 1.2 fusion.122
  488.3 1.9 broadcast_select_fusion
  491.6 1.6 pad_maximum_fusion.1
  493.2 4.1 copy.51
  498.4 1.2 convolution_multiply_fusion.30
  500.7 1.2 convolution_multiply_fusion.28
  501.9 51.9 %collective-permute-done.3 = f32[2,1024,256]{1,2,0:T(8,128)} collective-permute-done((f32[2,1024,256]{1,2,0:T(8,128)}, f32[2,1024,256]{1,2,0:T(8,128)}, u32[]{:S(2)}, u32[]{:S(2)}) %collective-permute-start.3) | collective-permute-done | bytes 2097184 | tf_op jit(solution)/shard_map/ppermute | solution.py:16
  553.8 2.9 select_add_fusion
  558.0 1.2 convolution_multiply_fusion.20
  560.2 1.2 convolution_multiply_fusion.24
  562.3 22.9 %collective-permute-done.4 = f32[2,512,256]{1,2,0:T(8,128)S(1)} collective-permute-done((f32[2,512,256]{1,2,0:T(8,128)S(1)}, f32[2,512,256]{1,2,0:T(8,128)S(1)}, u32[]{:S(2)}, u32[]{:S(2)}) %collective-permute-start.4) | collective-permute-done | bytes 1048608 | tf_op jit(solution)/shard_map/ppermute | solution.py:16
  586.5 2.3 collective-permute-start.5
  588.9 548.2 %all-reduce.3.cloned.1.call-done = f32[2,1024,256]{2,0,1:T(2,128)} async-done(((f32[2,1024,256]{2,0,1:T(2,128)}), f32[2,1024,256]{2,0,1:T(2,128)}) %all-reduce.3.cloned.1.call-update) | async-done | bytes 2097168
  (298 shorter events, 50.3 us)
Async XLA Ops:
  7.2 93.0 %copy-start = (bf16[64,1024]{1,0:T(8,128)(2,1)S(1)}, bf16[64,1024]{1,0:T(8,128)(2,1)}, u32[]{:S(2)}) copy-start(bf16[64,1024]{1,0:T(8,128)(2,1)} %param.6) | copy-start | bytes 393220
  7.2 93.0 %all-gather.5.cloned.1.call-start = ((), (), s32[]{:S(2)}) async-start(), calls=%async_computation.2 | async-start | bytes 2621440 | tf_op jit(solution)/shard_map/all_gather | solution.py:89
  7.2 43.0 %copy-start.35 = (bf16[256,256]{1,0:T(8,128)(2,1)S(1)}, bf16[256,256]{1,0:T(8,128)(2,1)}, u32[]{:S(2)}) copy-start(bf16[256,256]{1,0:T(8,128)(2,1)} %param.9) | copy-start | bytes 393220
  8.3 42.8 %copy-start.36 = (bf16[256,256]{1,0:T(8,128)(2,1)S(1)}, bf16[256,256]{1,0:T(8,128)(2,1)}, u32[]{:S(2)}) copy-start(bf16[256,256]{1,0:T(8,128)(2,1)} %param.10) | copy-start | bytes 393220
  8.3 8.3 collective-permute-start
  10.3 41.7 %copy-start.24 = (bf16[256,256]{1,0:T(8,128)(2,1)S(1)}, bf16[256,256]{1,0:T(8,128)(2,1)}, u32[]{:S(2)}) copy-start(bf16[256,256]{1,0:T(8,128)(2,1)} %param.8) | copy-start | bytes 393220
  10.4 42.5 %copy-start.92 = (u32[256]{0:T(256)S(1)}, u32[256]{0:T(256)}, u32[]{:S(2)}) copy-start(u32[256]{0:T(256)} %constant.137) | copy-start | bytes 3076
  10.4 43.8 %copy-start.91 = (s32[16]{0:T(128)S(1)}, s32[16]{0:T(128)}, u32[]{:S(2)}) copy-start(s32[16]{0:T(128)} %param.11) | copy-start | bytes 196
  17.9 25.8 %collective-permute-start.1 = (bf16[2,512,256]{2,1,0:T(8,128)(2,1)S(1)}, bf16[2,512,256]{2,1,0:T(8,128)(2,1)S(1)}, u32[]{:S(2)}, u32[]{:S(2)}) collective-permute-start(bf16[2,512,256]{2,1,0:T(8,128)(2,1)S(1)} %maximum_select_fusion.2), channel_id=1, source_target_pairs={{0,8},{4,12},{8,0},{12,4},{16,24},{20,28},{24,16},{28,20},{32,40},... | collective-permute-start | bytes 1572872 | tf_op jit(solution)/shard_map/ppermute | solution.py:16
  44.0 52.1 %collective-permute-start.2 = (bf16[2,1024,256]{2,1,0:T(8,128)(2,1)S(1)}, bf16[2,1024,256]{2,1,0:T(8,128)(2,1)S(1)}, u32[]{:S(2)}, u32[]{:S(2)}) collective-permute-start(bf16[2,1024,256]{2,1,0:T(8,128)(2,1)S(1)} %maximum_select_fusion.1), channel_id=1, source_target_pairs={{0,16},{4,20},{8,24},{12,28},{16,0},{20,4},{24,8},{28,12},{32,48},... | collective-permute-start | bytes 3145736 | tf_op jit(solution)/shard_map/ppermute | solution.py:16
  59.5 52.3 %copy-start.43 = (pred[16,4]{1,0:T(8,128)(4,1)}, pred[16,4]{1,0:T(8,128)(4,1)S(1)}, u32[]{:S(2)}) copy-start(pred[16,4]{1,0:T(8,128)(4,1)S(1)} %iota_compare_fusion) | copy-start | bytes 196
  99.6 8.4 copy-start.64
  100.1 14.8 %copy-start.63 = (f32[256]{0:T(256)}, f32[256]{0:T(256)S(1)}, u32[]{:S(2)}) copy-start(f32[256]{0:T(256)S(1)} %get-tuple-element.199) | copy-start | bytes 3076
  103.2 7.8 all-to-all-start
  108.0 304.4 %all-gather.3.cloned.1.call-start = ((), (), s32[]{:S(2)}) async-start(), calls=%async_computation.1 | async-start | bytes 1064960 | tf_op jit(solution)/shard_map/all_gather | solution.py:105
  114.7 1022.5 %all-reduce.3.cloned.1.call-start = ((), (), s32[]{:S(2)}) async-start(), calls=%async_computation.3 | async-start | bytes 4194304
  412.4 4.8 copy-start.9
  412.4 8.1 copy-start.90
  412.4 8.3 copy-start.34
  413.8 11.1 copy-start.12
  413.8 9.8 copy-start.89
  413.8 9.9 copy-start.33
  414.2 14.1 %copy-start.31 = (f32[16,1024]{1,0:T(8,128)}, f32[16,1024]{1,0:T(8,128)S(1)}, u32[]{:S(2)}) copy-start(f32[16,1024]{1,0:T(8,128)S(1)} %get-tuple-element.163) | copy-start | bytes 196612
  414.8 11.7 %copy-start.29 = (f32[16,1024]{1,0:T(8,128)}, f32[16,1024]{1,0:T(8,128)S(1)}, u32[]{:S(2)}) copy-start(f32[16,1024]{1,0:T(8,128)S(1)} %get-tuple-element.182) | copy-start | bytes 196612
  414.8 11.5 %copy-start.88 = (f32[16]{0:T(128)S(1)}, f32[16]{0:T(128)}, u32[]{:S(2)}) copy-start(f32[16]{0:T(128)} %get-tuple-element.160) | copy-start | bytes 196
  414.9 11.7 %copy-start.32 = (f32[16,2048]{1,0:T(8,128)S(1)}, f32[16,2048]{1,0:T(8,128)}, u32[]{:S(2)}) copy-start(f32[16,2048]{1,0:T(8,128)} %get-tuple-element.161) | copy-start | bytes 393220
  417.2 10.6 copy-start.45
  420.5 8.8 copy-start.87
  420.9 8.3 copy-start.49
  424.0 5.3 copy-start.52
  431.3 4.4 copy-start.2
  432.8 6.5 copy-start.56
  435.7 3.5 copy-start.82
  435.7 3.5 copy-start.83
  435.7 3.5 copy-start.53
  435.7 3.5 copy-start.86
  442.5 3.7 copy-start.57
  448.4 4.4 copy-start.7
  449.8 6.5 copy-start.59
  452.8 3.6 copy-start.78
  452.8 3.6 copy-start.79
  452.8 3.6 copy-start.46
  452.8 3.6 copy-start.84
  458.4 4.3 copy-start.4
  459.9 6.4 copy-start.61
  462.7 3.5 copy-start.42
  462.7 3.5 copy-start.47
  462.8 3.5 copy-start.77
  470.9 8.6 copy-start.38
  473.3 6.3 copy-start.40
  476.8 3.3 copy-start.67
  476.8 3.3 copy-start.72
  476.8 3.9 copy-start.21
  476.8 3.9 copy-start.58
  488.3 2.8 copy-start.48
  488.3 3.0 copy-start.37
  490.3 63.6 %collective-permute-start.3 = (f32[2,1024,256]{1,2,0:T(8,128)}, f32[2,1024,256]{1,2,0:T(8,128)}, u32[]{:S(2)}, u32[]{:S(2)}) collective-permute-start(f32[2,1024,256]{1,2,0:T(8,128)} %broadcast_select_fusion), channel_id=1, source_target_pairs={{0,16},{4,20},{8,24},{12,28},{16,0},{20,4},{24,8},{28,12},{32,48},... | collective-permute-start | bytes 6291464 | tf_op jit(solution)/shard_map/ppermute | solution.py:16
  497.3 3.4 copy-start.41
  557.0 3.2 copy-start.18
  557.0 4.4 copy-start.20
  557.0 28.3 %collective-permute-start.4 = (f32[2,512,256]{1,2,0:T(8,128)S(1)}, f32[2,512,256]{1,2,0:T(8,128)S(1)}, u32[]{:S(2)}, u32[]{:S(2)}) collective-permute-start(f32[2,512,256]{1,2,0:T(8,128)S(1)} %slice_select_fusion), channel_id=1, source_target_pairs={{0,8},{4,12},{8,0},{12,4},{16,24},{20,28},{24,16},{28,20},{32,40},... | collective-permute-start | bytes 3145736 | tf_op jit(solution)/shard_map/ppermute | solution.py:16
  562.3 575.9 %copy-start.44 = (pred[16,4]{1,0:T(8,128)(4,1)S(1)}, pred[16,4]{1,0:T(8,128)(4,1)}, u32[]{:S(2)}) copy-start(pred[16,4]{1,0:T(8,128)(4,1)} %copy-done.43) | copy-start | bytes 196
  586.5 555.5 %collective-permute-start.5 = (f32[2,256,256]{1,2,0:T(8,128)}, f32[2,256,256]{1,2,0:T(8,128)S(1)}, u32[]{:S(2)}, u32[]{:S(2)}) collective-permute-start(f32[2,256,256]{1,2,0:T(8,128)} %slice_select_fusion.1), channel_id=1, source_target_pairs={{0,4},{4,0},{8,12},{12,8},{16,20},{20,16},{24,28},{28,24},{32,36},... | collective-permute-start | bytes 1572872 | tf_op jit(solution)/shard_map/ppermute | solution.py:16
  1140.2 3.5 copy-start.1
  (39 other events, 72.9 us)
Sparse Core Ops, SparseCore 0:
  10.5 28.7 all-gather.4
  114.8 297.5 all-gather.2
  497.4 639.6 all-reduce.2
where the time goes:
time: 1150 us
  waiting for transfers between devices  973 us (85%)
  matrix products  60 us (5%)
  other arithmetic  48.8 us (4%)
  local copies, waits for them, and re-layouts  33.5 us (3%)
  starting transfers between devices  19.1 us (2%)
  between operations  15.5 us (1%)
    unnamed x4, waiting for transfers between devices  548 us
    all_gather x1, waiting for transfers between devices, body(): far_pair = lax.all_gather(picked_pair, 'context', axis=1, tiled=True)  284 us
    ppermute x6, waiting for transfers between devices, partner_2(): return lax.ppermute(value, axis, pairs)  140 us
    dot_general x25, matrix products, dot_rows(): lax.dot_general(left, right, (((1,), (1,)), ((), ())), preferred_element_...  36.3 us
  transfers between devices with their start and end apart: 10, of which 8 were waited for; matrix products, arithmetic and copies ran while one was open for 5% of the time, Pallas kernels for 0%

commit v1 on v0

v1 whole, which is shorter than its diff:
```python
import functools

import jax
import jax.numpy as jnp
from jax import lax
from jax.experimental import pallas as pl
from jax.experimental.pallas import tpu as pltpu
from jax.sharding import PartitionSpec as P

Z = 8
RATE = 16
BF = jnp.bfloat16
F32 = jnp.float32
MESH = pl.DeviceIdType.MESH
LOW = -1e30


def nn(a, b):
    return lax.dot_general(a, b, (((1,), (0,)), ((), ())), preferred_element_type=F32)


def nt(a, b):
    return lax.dot_general(a, b, (((1,), (1,)), ((), ())), preferred_element_type=F32)


def iota(shape, dim):
    return lax.broadcasted_iota(jnp.int32, shape, dim)


def place(rows, offset, zl):
    return 16 * (((rows & 15) - offset + zl + 16) & 15) + (rows >> 4)


def attn_kernel(
    nseg,
    off_ref, up_ref, w_ref, q_ref, k_ref, v_ref,
    rkv, rq,
    kvs, qts, ots, kv, qt, ot, up, pick, fk, ex, dp,
    m_s, l_s, d_s, f_s, dqt, fse, fre, sse, sre, dkv_s, rks, rqs,
    up_ss, up_rs, qt_ss, qt_rs, kv_ss, kv_rs, fw_ss, ot_ss, ot_rs,
    fa_ss, fa_rs, fb_ss, fb_rs, si_ss, si_rs, rk_ss, rk_rs, rq_ss, rq_rs,
):
    ctx = lax.axis_index("context")
    hd = lax.axis_index("heads")
    s = lax.div(ctx, Z)
    z = lax.rem(ctx, Z)
    xh = lax.div(hd, 2)
    c = lax.rem(hd, 2)
    zh = lax.div(z, 4)
    zl = lax.rem(z, 4)
    oc = 1 - c

    def dev(sv, zv, xv, cv):
        return {"context": sv * Z + zv, "heads": xv * 2 + cv}

    sibling = dev(s, z, xh, oc)
    partner = dev(s, z, 1 - xh, c)

    def peer(i):
        return dev(s, 4 * c + i, xh, zh)

    def far_seg(t):
        return lax.rem(s + t, nseg)

    def is_me(i):
        return jnp.logical_and(zh == c, zl == i)

    def rdma(src, dst, ss, rs, device):
        return pltpu.make_async_remote_copy(
            src_ref=src, dst_ref=dst, send_sem=ss, recv_sem=rs, device_id=device, device_id_type=MESH
        )

    def peer_send(src, dst, ss, rs, i):
        me = is_me(i)

        @pl.when(me)
        def _():
            pltpu.make_async_copy(src, dst, rs).start()

        @pl.when(jnp.logical_not(me))
        def _():
            rdma(src, dst, ss, rs, peer(i)).start()

    def peer_sent(src, ss, i):
        @pl.when(jnp.logical_not(is_me(i)))
        def _():
            rdma(src, src, ss, ss, peer(i)).wait_send()

    def arrived(dst, rs):
        pltpu.make_async_copy(dst, dst, rs).wait()

    bar = pltpu.get_barrier_semaphore()

    def hello(device):
        pl.semaphore_signal(bar, inc=1, device_id=device, device_id_type=MESH)

    for i in range(4):
        @pl.when(jnp.logical_not(is_me(i)))
        def _():
            hello(peer(i))
    hello(sibling)
    hello(partner)
    for t in range(1, nseg):
        for cc in range(2):
            hello(dev(far_seg(t), z, xh, cc))

    for b in range(4):
        qt[b, 64:128, :] = jnp.zeros((64, 256), BF)
        ot[b, 0:64, :] = jnp.zeros((64, 256), BF)
    pad = m_s.shape[0]
    m_s[...] = jnp.full(m_s.shape, LOW, F32)
    l_s[...] = jnp.zeros(l_s.shape, F32)
    d_s[...] = jnp.zeros(d_s.shape, F32)
    row = iota((256, 256), 1)
    col = iota((256, 256), 0)
    low_half = iota((256, 128), 1) < 64
    q_t = q_ref[...].astype(F32).T.astype(BF)
    perms = []
    for h in range(4):
        perm = (col == place(row, off_ref[hd * 4 + h], zl)).astype(F32).astype(BF)
        perms.append(perm)
        qts[h] = (nt(q_t[64 * h : 64 * h + 64, :], perm) * 0.125).astype(BF)
        lanes = slice(128 * (h // 2), 128 * (h // 2) + 128)
        k_h = nn(perm, k_ref[:, lanes])
        v_h = nn(perm, v_ref[:, lanes])
        if h % 2:
            k_h = pltpu.roll(k_h, 64, 1)
        else:
            v_h = pltpu.roll(v_h, 64, 1)
        kvs[h] = jnp.where(low_half, k_h, v_h).astype(BF)
    up[hd] = up_ref[...]

    pl.semaphore_wait(bar, 4 + 2 + 2 * (nseg - 1) - jnp.where(zh == c, 1, 0))

    rdma(up_ref, up.at[hd], up_ss.at[0], up_rs.at[0], partner).start()
    rdma(up_ref, up.at[hd], up_ss.at[1], up_rs.at[1], sibling).start()
    for i in range(4):
        peer_send(qts.at[i], qt.at[zl, 0:64, :], qt_ss.at[i], qt_rs.at[zl], i)
    for i in range(4):
        peer_send(kvs.at[i], kv.at[z], kv_ss.at[i], kv_rs.at[z], i)

    far_hd = (1 - xh) * 2 + c
    arrived(up.at[far_hd], up_rs.at[0])
    rdma(up.at[far_hd], up.at[far_hd], up_ss.at[2], up_rs.at[2], sibling).start()
    arrived(up.at[xh * 2 + oc], up_rs.at[1])
    arrived(up.at[(1 - xh) * 2 + oc], up_rs.at[2])
    a_t = nt(w_ref[...], up[...].reshape(256, up.shape[2])).astype(BF)
    for h in range(4):
        ots[h] = nt(a_t[64 * h : 64 * h + 64, :], perms[h]).astype(BF)
    for i in range(4):
        peer_send(ots.at[i], ot.at[zl, 64:128, :], ot_ss.at[i], ot_rs.at[zl], i)

    for i in range(4):
        arrived(qt.at[i, 0:64, :], qt_rs.at[i])

    def score_block(d):
        keys = kv[d]
        for b in range(4):
            st = nn(keys, qt[b])
            mb = jnp.max(st, axis=0, keepdims=True)
            e = jnp.exp(st - mb)
            ex[d, b] = e
            m_s[pl.ds(d, 1), 256 * b : 256 * b + 256] = mb
            l_s[pl.ds(d, 1), 256 * b : 256 * b + 256] = jnp.sum(e, axis=0, keepdims=True)

    def own_block(i, carry):
        d = 4 * c + lax.rem(zl + i, 4)
        arrived(kv.at[d], kv_rs.at[d])
        rdma(kv.at[d], kv.at[d], fw_ss.at[i], kv_rs.at[d], sibling).start()
        score_block(d)
        return carry

    lax.fori_loop(0, 4, own_block, 0)

    for i in range(4):
        pick[16 * i : 16 * i + 16, :] = kv[4 * c + i, 16 * i : 16 * i + 16, :]
    for t in range(1, nseg):
        for cc in range(2):
            rdma(
                pick, fk.at[s, c], fa_ss.at[t, cc], fa_rs.at[s, c], dev(far_seg(t), z, xh, cc)
            ).start()

    def other_block(i, carry):
        d = 4 * oc + lax.rem(zl + i, 4)
        arrived(kv.at[d], kv_rs.at[d])
        score_block(d)
        return carry

    lax.fori_loop(0, 4, other_block, 0)
    for d in range(Z):
        i = d % 4
        fk[s, d // 4, 16 * i : 16 * i + 16, :] = kv[d, 16 * i : 16 * i + 16, :]

    for i in range(4):
        arrived(ot.at[i, 64:128, :], ot_rs.at[i])

    def dprob_block(d, carry):
        keys = kv[d]
        for b in range(4):
            g = nn(keys, ot[b])
            dp[d, b] = g
            d_s[pl.ds(d, 1), 256 * b : 256 * b + 256] = jnp.sum(ex[d, b] * g, axis=0, keepdims=True)
        return carry

    lax.fori_loop(0, Z, dprob_block, 0)

    lane = iota((1, 128), 1)
    mine = [jnp.logical_and(lane >= 16 * b, lane < 16 * b + 16) for b in range(4)]

    def gather_lanes(parts):
        out = jnp.zeros(parts[0].shape, parts[0].dtype)
        for b in range(4):
            out = jnp.where(mine[b], parts[b], out)
        return out

    q_far = gather_lanes([qt[b, :, 0:128].astype(F32) for b in range(4)]).astype(BF)
    o_far = gather_lanes([ot[b, :, 0:128].astype(F32) for b in range(4)]).astype(BF)
    for t in range(1, nseg):
        for cc in range(2):
            arrived(fk.at[far_seg(t), cc], fa_rs.at[far_seg(t), cc])
    far_keys = fk[...].reshape(nseg * 128, 128)
    st = nn(far_keys, q_far)
    m_far = jnp.max(st, axis=0, keepdims=True)
    e_far = jnp.exp(st - m_far)
    l_far = jnp.sum(e_far, axis=0, keepdims=True)
    g_far = nn(far_keys, o_far)
    d_far = jnp.sum(e_far * g_far, axis=0, keepdims=True)
    for b in range(4):
        lanes = slice(256 * b, 256 * b + 128)
        m_s[Z : Z + 1, lanes] = jnp.where(mine[b], m_far, LOW)
        l_s[Z : Z + 1, lanes] = jnp.where(mine[b], l_far, 0.0)
        d_s[Z : Z + 1, lanes] = jnp.where(mine[b], d_far, 0.0)

    m_all = m_s[...]
    m_row = jnp.max(m_all, axis=0, keepdims=True)
    lse = m_row + jnp.log(jnp.sum(l_s[...] * jnp.exp(m_all - m_row), axis=0, keepdims=True))
    factor = jnp.exp(m_all - lse)
    f_s[0:pad, :] = factor
    delta = jnp.sum(factor * d_s[...], axis=0, keepdims=True)
    f_s[pad : pad + 1, :] = delta

    f_far = gather_lanes([factor[Z : Z + 1, 256 * b : 256 * b + 128] for b in range(4)])
    delta_far = gather_lanes([delta[:, 256 * b : 256 * b + 128] for b in range(4)])
    p_far = e_far * f_far
    ds_far = (p_far * (g_far - delta_far)).astype(BF)
    dkv_far = nt(ds_far, q_far) + nt(p_far.astype(BF), o_far)
    fse[...] = dkv_far.astype(BF).reshape(nseg, 2, 64, 128)
    for t in range(1, nseg):
        for cc in range(2):
            rdma(
                fse.at[far_seg(t), cc], fre.at[s, c], fb_ss.at[t, cc], fb_rs.at[s, c],
                dev(far_seg(t), z, xh, cc),
            ).start()
    rdma(fse.at[s, oc], fre.at[s, c], fb_ss.at[0, 0], fb_rs.at[s, c], sibling).start()
    fre[s, c] = fse[s, c]
    keys_t = far_keys.astype(F32).T[0:64, :].astype(BF)
    dq_far = nn(keys_t, ds_far)
    for b in range(4):
        dqt[b, :, 0:128] = jnp.where(mine[b], dq_far, 0.0)
        dqt[b, :, 128:256] = jnp.zeros((64, 128), F32)

    def grad_block(d):
        kt = kv[d].astype(F32).T[0:64, :].astype(BF)
        acc = jnp.zeros((256, 128), F32)
        for b in range(4):
            lanes = slice(256 * b, 256 * b + 256)
            p = ex[d, b] * f_s[pl.ds(d, 1), lanes]
            ds = (p * (dp[d, b] - f_s[pad : pad + 1, lanes])).astype(BF)
            acc = acc + nt(ds, qt[b]) + nt(p.astype(BF), ot[b])
            dqt[b] = dqt[b] + nn(kt, ds)
        return acc

    def sibling_grads(i, carry):
        sse[i] = grad_block(4 * oc + i).astype(BF)
        rdma(sse.at[i], sre.at[i], si_ss.at[i], si_rs.at[i], sibling).start()
        return carry

    lax.fori_loop(0, 4, sibling_grads, 0)
    for t in range(1, nseg):
        for cc in range(2):
            arrived(fre.at[far_seg(t), cc], fb_rs.at[far_seg(t), cc])
    arrived(fre.at[s, oc], fb_rs.at[s, oc])
    fsum = jnp.zeros((64, 128), F32)
    for t in range(nseg):
        for cc in range(2):
            fsum = fsum + fre[t, cc].astype(F32)
    for i in range(4):
        acc = grad_block(4 * c + i)
        arrived(sre.at[i], si_rs.at[i])
        dkv_s[...] = acc + sre[i].astype(F32)
        rows = slice(16 * i, 16 * i + 16)
        dkv_s[rows, :] = dkv_s[rows, :] + fsum[rows, :]
        rks[i] = dkv_s[...].astype(BF)
        peer_send(rks.at[i], rkv.at[zl], rk_ss.at[i], rk_rs.at[zl], i)
    for i in range(4):
        rqs[i] = (dqt[i] * 0.125).astype(BF)
        peer_send(rqs.at[i], rq.at[zl], rq_ss.at[i], rq_rs.at[zl], i)

    for i in range(4):
        arrived(rkv.at[i], rk_rs.at[i])
        arrived(rq.at[i], rq_rs.at[i])

    rdma(up_ref, up_ref, up_ss.at[0], up_ss.at[0], partner).wait_send()
    rdma(up_ref, up_ref, up_ss.at[1], up_ss.at[1], sibling).wait_send()
    rdma(up_ref, up_ref, up_ss.at[2], up_ss.at[2], sibling).wait_send()
    for i in range(4):
        peer_sent(qts.at[i], qt_ss.at[i], i)
        peer_sent(kvs.at[i], kv_ss.at[i], i)
        peer_sent(ots.at[i], ot_ss.at[i], i)
        peer_sent(rks.at[i], rk_ss.at[i], i)
        peer_sent(rqs.at[i], rq_ss.at[i], i)
        rdma(kvs.at[i], kvs.at[i], fw_ss.at[i], fw_ss.at[i], sibling).wait_send()
        rdma(sse.at[i], sse.at[i], si_ss.at[i], si_ss.at[i], sibling).wait_send()
    for t in range(1, nseg):
        for cc in range(2):
            device = dev(far_seg(t), z, xh, cc)
            rdma(pick, pick, fa_ss.at[t, cc], fa_ss.at[t, cc], device).wait_send()
            rdma(pick, pick, fb_ss.at[t, cc], fb_ss.at[t, cc], device).wait_send()
    rdma(pick, pick, fb_ss.at[0, 0], fb_ss.at[0, 0], sibling).wait_send()


def home_kernel(off_ref, rkv, rq, dq_ref, dk_ref, dv_ref):
    ctx = lax.axis_index("context")
    hd = lax.axis_index("heads")
    zl = lax.rem(ctx, 4)
    row = iota((256, 256), 0)
    col = iota((256, 256), 1)
    low_half = iota((256, 128), 1) < 64
    for pair in range(2):
        lanes = slice(128 * pair, 128 * pair + 128)
        both_q = rq[2 * pair : 2 * pair + 2].reshape(128, 256)
        back, queries = [], []
        for h in (2 * pair, 2 * pair + 1):
            perm = (col == place(row, off_ref[hd * 4 + h], zl)).astype(F32).astype(BF)
            back.append(nn(perm, rkv[h]))
            queries.append(nt(perm, both_q))
        dq_ref[:, lanes] = jnp.where(low_half, queries[0], queries[1]).astype(BF)
        dk_ref[:, lanes] = jnp.where(low_half, back[0], pltpu.roll(back[1], 64, 1)).astype(BF)
        dv_ref[:, lanes] = jnp.where(low_half, pltpu.roll(back[0], 64, 1), back[1]).astype(BF)


def solution(mesh):
    nseg = mesh.shape["context"] // Z
    vmem = pl.BlockSpec(memory_space=pltpu.VMEM)
    smem = pl.BlockSpec(memory_space=pltpu.SMEM)
    dma = pltpu.SemaphoreType.DMA
    nq = 1024

    def body(upstream, out_weight, query_rows, key_rows, value_rows, head_offsets):
        width = upstream.shape[1]
        rkv, rq = pl.pallas_call(
            functools.partial(attn_kernel, nseg),
            out_shape=(
                jax.ShapeDtypeStruct((4, 256, 128), BF),
                jax.ShapeDtypeStruct((4, 64, 256), BF),
            ),
            in_specs=[smem] + [vmem] * 5,
            out_specs=(vmem, vmem),
            scratch_shapes=[
                pltpu.VMEM((4, 256, 128), BF),
                pltpu.VMEM((4, 64, 256), BF),
                pltpu.VMEM((4, 64, 256), BF),
                pltpu.VMEM((Z, 256, 128), BF),
                pltpu.VMEM((4, 128, 256), BF),
                pltpu.VMEM((4, 128, 256), BF),
                pltpu.VMEM((4, 64, width), BF),
                pltpu.VMEM((64, 128), BF),
                pltpu.VMEM((nseg, 2, 64, 128), BF),
                pltpu.VMEM((Z, 4, 256, 256), F32),
                pltpu.VMEM((Z, 4, 256, 256), F32),
                pltpu.VMEM((16, nq), F32),
                pltpu.VMEM((16, nq), F32),
                pltpu.VMEM((16, nq), F32),
                pltpu.VMEM((24, nq), F32),
                pltpu.VMEM((4, 64, 256), F32),
                pltpu.VMEM((nseg, 2, 64, 128), BF),
                pltpu.VMEM((nseg, 2, 64, 128), BF),
                pltpu.VMEM((4, 256, 128), BF),
                pltpu.VMEM((4, 256, 128), BF),
                pltpu.VMEM((256, 128), F32),
                pltpu.VMEM((4, 256, 128), BF),
                pltpu.VMEM((4, 64, 256), BF),
                dma((3,)), dma((3,)),
                dma((4,)), dma((4,)),
                dma((4,)), dma((Z,)), dma((4,)),
                dma((4,)), dma((4,)),
                dma((nseg, 2)), dma((nseg, 2)),
                dma((nseg, 2)), dma((nseg, 2)),
                dma((4,)), dma((4,)),
                dma((4,)), dma((4,)),
                dma((4,)), dma((4,)),
            ],
            compiler_params=pltpu.CompilerParams(
                collective_id=0, has_side_effects=True, vmem_limit_bytes=48 * 1024 * 1024
            ),
            name="attn",
        )(head_offsets, upstream, out_weight, query_rows, key_rows, value_rows)
        block = jax.ShapeDtypeStruct(query_rows.shape, BF)
        return pl.pallas_call(
            home_kernel,
            out_shape=(block, block, block),
            in_specs=[smem, vmem, vmem],
            out_specs=(vmem, vmem, vmem),
            name="home",
        )(head_offsets, rkv, rq)

    return jax.shard_map(
        body,
        mesh=mesh,
        in_specs=(
            P(("context", "heads"), None),
            P("heads", None),
            P("context", "heads"),
            P("context", "heads"),
            P("context", "heads"),
            P(),
        ),
        out_specs=(P("context", "heads"), P("context", "heads"), P("context", "heads")),
        check_vma=False,
    )
```

time: 1150 us -> 56.9 us (0.05)
  the two profiles are of different devices: /device:TPU:4 before, /device:TPU:1 now
where the time goes in v1:
time: 56.9 us; the launch traced here: 56.6 us
  Pallas kernels  49.3 us (87%)
  local copies, waits for them, and re-layouts  6.63 us (12%)
  between operations  0.66 us (1%)
    pallas_call x1, Pallas kernels, body(): pl.pallas_call(functools.partial(attn_kernel, nseg), out_shape=(jax.Shape...  47.2 us
    unnamed x16, local copies, waits for them, and re-layouts  6.63 us
    pallas_call x1, Pallas kernels, body(): pl.pallas_call(home_kernel, out_shape=(block, block, block), in_specs=[sm...  2.18 us

profile of v1, /device:TPU:1, one launch (start us, length us, event | category | flops | bytes accessed | tf_op | source)
XLA Modules:
  0.0 56.6 jit_solution(5760033557383019427)
XLA Ops:
  0.6 0.0 copy-start
  0.6 1.0 %copy-done = bf16[256,1024]{1,0:T(8,128)(2,1)S(1)} copy-done((bf16[256,1024]{1,0:T(8,128)(2,1)S(1)}, bf16[256,1024]{1,0:T(8,128)(2,1)}, u32[]{:S(2)}) %copy-start) | copy-done | bytes 524312
  1.7 0.0 copy-start.3
  1.7 0.9 %copy-done.3 = bf16[64,1024]{1,0:T(8,128)(2,1)S(1)} copy-done((bf16[64,1024]{1,0:T(8,128)(2,1)S(1)}, bf16[64,1024]{1,0:T(8,128)(2,1)}, u32[]{:S(2)}) %copy-start.3) | copy-done | bytes 131096
  2.6 0.0 copy-start.4
  2.6 0.9 %copy-done.4 = bf16[256,256]{1,0:T(8,128)(2,1)S(1)} copy-done((bf16[256,256]{1,0:T(8,128)(2,1)S(1)}, bf16[256,256]{1,0:T(8,128)(2,1)}, u32[]{:S(2)}) %copy-start.4) | copy-done | bytes 131096
  3.5 0.0 copy-start.5
  3.5 0.9 %copy-done.5 = bf16[256,256]{1,0:T(8,128)(2,1)S(1)} copy-done((bf16[256,256]{1,0:T(8,128)(2,1)S(1)}, bf16[256,256]{1,0:T(8,128)(2,1)}, u32[]{:S(2)}) %copy-start.5) | copy-done | bytes 131096
  4.4 0.0 copy-start.6
  4.4 0.9 %copy-done.6 = bf16[256,256]{1,0:T(8,128)(2,1)S(1)} copy-done((bf16[256,256]{1,0:T(8,128)(2,1)S(1)}, bf16[256,256]{1,0:T(8,128)(2,1)}, u32[]{:S(2)}) %copy-start.6) | copy-done | bytes 131096
  5.3 0.0 copy-start.7
  5.3 0.7 %copy-done.7 = s32[16]{0:T(128)S(1)} copy-done((s32[16]{0:T(128)S(1)}, s32[16]{0:T(128)}, u32[]{:S(2)}) %copy-start.7) | copy-done | bytes 88
  5.9 47.2 %attn.1 = (bf16[4,256,128]{2,1,0:T(8,128)(2,1)S(1)}, bf16[4,64,256]{2,1,0:T(8,128)(2,1)S(1)}) custom-call(s32[16]{0:T(128)S(1)} %copy-done.7, bf16[64,1024]{1,0:T(8,128)(2,1)S(1)} %copy-done.3, bf16[256,1024]{1,0:T(8,128)(2,1)S(1)} %copy-done, bf16[256,256]{1,0:T(8,128)(2,1)S(1)} %copy-done.4, bf16[256,256]{1,0:T(8,128)(2,1)S(1)} %copy-done.5, ...), custom_call_target="tpu_custom_call" | custom-call | tf_op jit(solution)/shard_map/attn/pallas_call | solution.py:351
  53.1 0.0 copy-start.1
  53.1 0.7 %copy-done.1 = bf16[4,256,128]{2,1,0:T(8,128)(2,1)} copy-done((bf16[4,256,128]{2,1,0:T(8,128)(2,1)}, bf16[4,256,128]{2,1,0:T(8,128)(2,1)S(1)}, u32[]{:S(2)}) %copy-start.1) | copy-done | bytes 262168
  53.8 0.0 copy-start.2
  53.8 0.6 %copy-done.2 = bf16[4,64,256]{2,1,0:T(8,128)(2,1)} copy-done((bf16[4,64,256]{2,1,0:T(8,128)(2,1)}, bf16[4,64,256]{2,1,0:T(8,128)(2,1)S(1)}, u32[]{:S(2)}) %copy-start.2) | copy-done | bytes 131096
  54.5 2.2 %home.1 = (bf16[256,256]{1,0:T(8,128)(2,1)}, bf16[256,256]{1,0:T(8,128)(2,1)}, bf16[256,256]{1,0:T(8,128)(2,1)}) custom-call(s32[16]{0:T(128)} %off_ref.3, bf16[4,256,128]{2,1,0:T(8,128)(2,1)} %copy-done.1, bf16[4,64,256]{2,1,0:T(8,128)(2,1)} %copy-done.2), custom_call_target="tpu_custom_call" | custom-call | tf_op jit(solution)/shard_map/home/pallas_call | solution.py:399
Async XLA Ops:
  0.6 1.0 %copy-start = (bf16[256,1024]{1,0:T(8,128)(2,1)S(1)}, bf16[256,1024]{1,0:T(8,128)(2,1)}, u32[]{:S(2)}) copy-start(bf16[256,1024]{1,0:T(8,128)(2,1)} %w_ref.1) | copy-start | bytes 1572868
  1.7 0.9 %copy-start.3 = (bf16[64,1024]{1,0:T(8,128)(2,1)S(1)}, bf16[64,1024]{1,0:T(8,128)(2,1)}, u32[]{:S(2)}) copy-start(bf16[64,1024]{1,0:T(8,128)(2,1)} %up_ref.1) | copy-start | bytes 393220
  2.6 0.9 %copy-start.4 = (bf16[256,256]{1,0:T(8,128)(2,1)S(1)}, bf16[256,256]{1,0:T(8,128)(2,1)}, u32[]{:S(2)}) copy-start(bf16[256,256]{1,0:T(8,128)(2,1)} %q_ref.1) | copy-start | bytes 393220
  3.5 0.9 %copy-start.5 = (bf16[256,256]{1,0:T(8,128)(2,1)S(1)}, bf16[256,256]{1,0:T(8,128)(2,1)}, u32[]{:S(2)}) copy-start(bf16[256,256]{1,0:T(8,128)(2,1)} %k_ref.1) | copy-start | bytes 393220
  4.4 0.9 %copy-start.6 = (bf16[256,256]{1,0:T(8,128)(2,1)S(1)}, bf16[256,256]{1,0:T(8,128)(2,1)}, u32[]{:S(2)}) copy-start(bf16[256,256]{1,0:T(8,128)(2,1)} %v_ref.1) | copy-start | bytes 393220
  5.3 0.7 %copy-start.7 = (s32[16]{0:T(128)S(1)}, s32[16]{0:T(128)}, u32[]{:S(2)}) copy-start(s32[16]{0:T(128)} %off_ref.3) | copy-start | bytes 196
  53.1 0.7 %copy-start.1 = (bf16[4,256,128]{2,1,0:T(8,128)(2,1)}, bf16[4,256,128]{2,1,0:T(8,128)(2,1)S(1)}, u32[]{:S(2)}) copy-start(bf16[4,256,128]{2,1,0:T(8,128)(2,1)S(1)} %get-tuple-element.5.rkv) | copy-start | bytes 786436
  53.8 0.6 %copy-start.2 = (bf16[4,64,256]{2,1,0:T(8,128)(2,1)}, bf16[4,64,256]{2,1,0:T(8,128)(2,1)S(1)}, u32[]{:S(2)}) copy-start(bf16[4,64,256]{2,1,0:T(8,128)(2,1)S(1)} %get-tuple-element.6.rq) | copy-start | bytes 393220

commit v2 on v1

v2 whole, which is shorter than its diff:
```python
import functools

import jax
import jax.numpy as jnp
from jax import lax
from jax.experimental import pallas as pl
from jax.experimental.pallas import tpu as pltpu
from jax.sharding import PartitionSpec as P

Z = 8
RATE = 16
BF = jnp.bfloat16
F32 = jnp.float32
MESH = pl.DeviceIdType.MESH
LOW = -1e30


def nn(a, b):
    return lax.dot_general(a, b, (((1,), (0,)), ((), ())), preferred_element_type=F32)


def nt(a, b):
    return lax.dot_general(a, b, (((1,), (1,)), ((), ())), preferred_element_type=F32)


def iota(shape, dim):
    return lax.broadcasted_iota(jnp.int32, shape, dim)


def place(rows, offset, zl):
    return 16 * (((rows & 15) - offset + zl + 16) & 15) + (rows >> 4)


def attn_kernel(
    nseg,
    off_h, up_h, w_h, q_h, k_h, v_h,
    rkv, rq, rf,
    off_ref, w_ref, q_ref, k_ref, v_ref,
    kvs, qts, ots, kv, kt, qt, ot, up, pick, fk, fkt, ex, dp,
    m_s, l_s, f_s, fe, fds, acc_s, fse, fre, sse, sre, rks, rqs, rfs,
    in_s, up_ss, up_rs, qt_ss, qt_rs, kv_ss, kv_rs, fw_ss, ot_ss, ot_rs, pk_ss, pk_rs,
    fa_ss, fa_rs, fb_ss, fb_rs, si_ss, si_rs, rk_ss, rk_rs, rq_ss, rq_rs, rf_ss, rf_rs,
):
    ctx = lax.axis_index("context")
    hd = lax.axis_index("heads")
    s = lax.div(ctx, Z)
    z = lax.rem(ctx, Z)
    xh = lax.div(hd, 2)
    c = lax.rem(hd, 2)
    zh = lax.div(z, 4)
    zl = lax.rem(z, 4)
    oc = 1 - c

    def dev(sv, zv, xv, cv):
        return {"context": sv * Z + zv, "heads": xv * 2 + cv}

    sibling = dev(s, z, xh, oc)
    partner = dev(s, z, 1 - xh, c)

    def peer(i):
        return dev(s, 4 * c + i, xh, zh)

    def far_seg(t):
        return lax.rem(s + t, nseg)

    def is_me(i):
        return jnp.logical_and(zh == c, zl == i)

    def rdma(src, dst, ss, rs, device):
        return pltpu.make_async_remote_copy(
            src_ref=src, dst_ref=dst, send_sem=ss, recv_sem=rs, device_id=device, device_id_type=MESH
        )

    def peer_send(src, dst, ss, rs, i):
        me = is_me(i)

        @pl.when(me)
        def _():
            pltpu.make_async_copy(src, dst, rs).start()

        @pl.when(jnp.logical_not(me))
        def _():
            rdma(src, dst, ss, rs, peer(i)).start()

    def peer_sent(src, ss, i):
        @pl.when(jnp.logical_not(is_me(i)))
        def _():
            rdma(src, src, ss, ss, peer(i)).wait_send()

    def arrived(dst, rs):
        pltpu.make_async_copy(dst, dst, rs).wait()

    def order(j):
        return lax.rem(zl + j, 4)

    bar = pltpu.get_barrier_semaphore()

    def hello(device):
        pl.semaphore_signal(bar, inc=1, device_id=device, device_id_type=MESH)

    for i in range(4):
        @pl.when(jnp.logical_not(is_me(i)))
        def _():
            hello(peer(i))
    hello(sibling)
    hello(partner)
    for t in range(1, nseg):
        for cc in range(2):
            hello(dev(far_seg(t), z, xh, cc))

    loads = [
        pltpu.make_async_copy(a, b, in_s.at[n])
        for n, (a, b) in enumerate(
            ((off_h, off_ref), (q_h, q_ref), (k_h, k_ref), (v_h, v_ref), (up_h, up.at[hd]), (w_h, w_ref))
        )
    ]
    for load in loads:
        load.start()

    for b in range(4):
        qt[b, 64:128, :] = jnp.zeros((64, 256), BF)
        ot[b, 0:64, :] = jnp.zeros((64, 256), BF)
    m_s[...] = jnp.full(m_s.shape, LOW, F32)
    l_s[...] = jnp.zeros(l_s.shape, F32)
    row = iota((256, 256), 1)
    col = iota((256, 256), 0)
    low_half = iota((256, 128), 1) < 64
    lane = iota((1, 128), 1)

    for load in loads[:4]:
        load.wait()
    q_t = q_ref[...].astype(F32).T.astype(BF)
    perms = []
    for h in range(4):
        perm = (col == place(row, off_ref[hd * 4 + h], zl)).astype(F32).astype(BF)
        perms.append(perm)
        qts[h] = (nt(q_t[64 * h : 64 * h + 64, :], perm) * 0.125).astype(BF)
        lanes = slice(128 * (h // 2), 128 * (h // 2) + 128)
        k_p = nn(perm, k_ref[:, lanes])
        v_p = nn(perm, v_ref[:, lanes])
        if h % 2:
            k_p = pltpu.roll(k_p, 64, 1)
        else:
            v_p = pltpu.roll(v_p, 64, 1)
        kvs[h] = jnp.where(low_half, k_p, v_p).astype(BF)
    loads[4].wait()

    pl.semaphore_wait(bar, 4 + 2 + 2 * (nseg - 1) - jnp.where(zh == c, 1, 0))

    picked = pl.ds(pl.multiple_of(16 * zl, 16), 16)
    rdma(up.at[hd], up.at[hd], up_ss.at[0], up_rs.at[0], partner).start()
    rdma(up.at[hd], up.at[hd], up_ss.at[1], up_rs.at[1], sibling).start()
    for j in range(4):
        i = order(j)
        peer_send(kvs.at[i, picked, :], pick.at[picked, :], pk_ss.at[i], pk_rs.at[zl], i)
    for j in range(4):
        i = order(j)
        peer_send(qts.at[i], qt.at[zl, 0:64, :], qt_ss.at[i], qt_rs.at[zl], i)
    for j in range(4):
        i = order(j)
        peer_send(kvs.at[i], kv.at[z], kv_ss.at[i], kv_rs.at[z], i)

    for i in range(4):
        arrived(pick.at[16 * i : 16 * i + 16, :], pk_rs.at[i])
    for t in range(1, nseg):
        for cc in range(2):
            rdma(
                pick, fk.at[s, c], fa_ss.at[t, cc], fa_rs.at[s, c], dev(far_seg(t), z, xh, cc)
            ).start()
    rdma(pick, fk.at[s, c], fa_ss.at[0, 0], fa_rs.at[s, c], sibling).start()
    fk[s, c] = pick[...]

    far_hd = (1 - xh) * 2 + c
    arrived(up.at[far_hd], up_rs.at[0])
    rdma(up.at[far_hd], up.at[far_hd], up_ss.at[2], up_rs.at[2], sibling).start()
    arrived(up.at[xh * 2 + oc], up_rs.at[1])
    loads[5].wait()
    arrived(up.at[(1 - xh) * 2 + oc], up_rs.at[2])
    a_t = nt(w_ref[...], up[...].reshape(256, up.shape[2])).astype(BF)
    for h in range(4):
        ots[h] = nt(a_t[64 * h : 64 * h + 64, :], perms[h]).astype(BF)
    for j in range(4):
        i = order(j)
        peer_send(ots.at[i], ot.at[zl, 64:128, :], ot_ss.at[i], ot_rs.at[zl], i)

    for i in range(4):
        arrived(qt.at[i, 0:64, :], qt_rs.at[i])

    def score_block(d):
        keys = kv[d]
        kt[d] = keys.astype(F32).T[0:64, :].astype(BF)
        for b in range(4):
            st = nn(keys, qt[b])
            mb = jnp.max(st, axis=0, keepdims=True)
            e = jnp.exp(st - mb)
            ex[d, b] = e
            m_s[b, pl.ds(d, 1), :] = mb
            l_s[b, pl.ds(d, 1), :] = jnp.sum(e, axis=0, keepdims=True)

    def own_block(j, carry):
        i = lax.rem(zl + 4 - j, 4)
        d = 4 * c + i
        arrived(kv.at[d], kv_rs.at[d])
        rdma(kv.at[d], kv.at[d], fw_ss.at[i], kv_rs.at[d], sibling).start()
        score_block(d)
        return carry

    def other_block(j, carry):
        d = 4 * oc + lax.rem(zl + 4 - j, 4)
        arrived(kv.at[d], kv_rs.at[d])
        score_block(d)
        return carry

    lax.fori_loop(0, 4, own_block, 0)
    lax.fori_loop(0, 4, other_block, 0)

    def mine(b):
        return jnp.logical_and(lane >= 16 * b, lane < 16 * b + 16)

    def gather_lanes(parts):
        out = jnp.zeros(parts[0].shape, parts[0].dtype)
        for b in range(4):
            out = jnp.where(mine(b), parts[b], out)
        return out

    q_far = gather_lanes([qt[b, :, 0:128].astype(F32) for b in range(4)]).astype(BF)
    for t in range(1, nseg):
        for cc in range(2):
            arrived(fk.at[far_seg(t), cc], fa_rs.at[far_seg(t), cc])
    arrived(fk.at[s, oc], fa_rs.at[s, oc])
    far_keys = fk[...].reshape(nseg * 128, 128)
    fkt[...] = far_keys.astype(F32).T[0:64, :].astype(BF)
    st = nn(far_keys, q_far)
    m_far = jnp.max(st, axis=0, keepdims=True)
    e_far = jnp.exp(st - m_far)
    fe[...] = e_far
    l_far = jnp.sum(e_far, axis=0, keepdims=True)
    for b in range(4):
        m_s[b, Z : Z + 1, 0:128] = jnp.where(mine(b), m_far, LOW)
        l_s[b, Z : Z + 1, 0:128] = jnp.where(mine(b), l_far, 0.0)
    for b in range(4):
        m_all = m_s[b]
        m_row = jnp.max(m_all, axis=0, keepdims=True)
        lse = m_row + jnp.log(jnp.sum(l_s[b] * jnp.exp(m_all - m_row), axis=0, keepdims=True))
        f_s[b] = jnp.exp(m_all - lse)
    fe[...] = fe[...] * gather_lanes([f_s[b, Z : Z + 1, 0:128] for b in range(4)])

    for b in range(4):
        arrived(ot.at[b, 64:128, :], ot_rs.at[b])
    o_far = gather_lanes([ot[b, :, 0:128].astype(F32) for b in range(4)]).astype(BF)
    g_far = nn(fk[...].reshape(nseg * 128, 128), o_far)
    fds[...] = g_far
    far_delta = jnp.sum(fe[...] * g_far, axis=0, keepdims=True)

    def dprob_block(d, total):
        keys = kv[d]
        out = []
        for b in range(4):
            g = nn(keys, ot[b])
            dp[d, b] = g
            part = jnp.sum(ex[d, b] * g, axis=0, keepdims=True)
            out.append(total[b] + f_s[b, pl.ds(d, 1), :] * part)
        return tuple(out)

    delta = lax.fori_loop(0, Z, dprob_block, tuple(jnp.zeros((1, 256), F32) for _ in range(4)))
    zero_row = jnp.zeros((1, 128), F32)
    delta = [
        delta[b] + jnp.concatenate([jnp.where(mine(b), far_delta, 0.0), zero_row], axis=1)
        for b in range(4)
    ]
    for b in range(4):
        l_s[b, 0:1, :] = delta[b]

    p_far = fe[...]
    ds_far = (p_far * (fds[...] - gather_lanes([delta[b][:, 0:128] for b in range(4)]))).astype(BF)
    dkv_far = nt(ds_far, q_far) + nt(p_far.astype(BF), o_far)
    fse[...] = dkv_far.astype(BF).reshape(nseg, 2, 64, 128)
    for t in range(1, nseg):
        for cc in range(2):
            rdma(
                fse.at[far_seg(t), cc], fre.at[s, c], fb_ss.at[t, cc], fb_rs.at[s, c],
                dev(far_seg(t), z, xh, cc),
            ).start()
    rdma(fse.at[s, oc], fre.at[s, c], fb_ss.at[0, 0], fb_rs.at[s, c], sibling).start()
    fre[s, c] = fse[s, c]
    dq_far = nn(fkt[...], ds_far)
    for b in range(4):
        acc_s[b, :, 0:128] = jnp.where(mine(b), dq_far, 0.0)
        acc_s[b, :, 128:256] = jnp.zeros((64, 128), F32)

    def grad_block(d):
        grads = jnp.zeros((256, 128), F32)
        keys_t = kt[d]
        for b in range(4):
            p = ex[d, b] * f_s[b, pl.ds(d, 1), :]
            ds = (p * (dp[d, b] - l_s[b, 0:1, :])).astype(BF)
            grads = grads + nt(ds, qt[b]) + nt(p.astype(BF), ot[b])
            acc_s[b] = acc_s[b] + nn(keys_t, ds)
        return grads

    def pair_block(n, carry):
        i = lax.rem(zl + n, 4)
        sse[i] = grad_block(4 * oc + i).astype(BF)
        rdma(sse.at[i], sre.at[i], si_ss.at[i], si_rs.at[i], sibling).start()
        grads = grad_block(4 * c + i)
        arrived(sre.at[i], si_rs.at[i])
        rks[i] = (grads + sre[i].astype(F32)).astype(BF)
        peer_send(rks.at[i], rkv.at[zl], rk_ss.at[i], rk_rs.at[zl], i)
        return carry

    lax.fori_loop(0, 4, pair_block, 0)
    for j in range(4):
        b = order(j)
        rqs[b] = (acc_s[b] * 0.125).astype(BF)
        peer_send(rqs.at[b], rq.at[zl], rq_ss.at[b], rq_rs.at[zl], b)

    for t in range(1, nseg):
        for cc in range(2):
            arrived(fre.at[far_seg(t), cc], fb_rs.at[far_seg(t), cc])
    arrived(fre.at[s, oc], fb_rs.at[s, oc])
    fsum = jnp.zeros((64, 128), F32)
    for t in range(nseg):
        for cc in range(2):
            fsum = fsum + fre[t, cc].astype(F32)
    for i in range(4):
        rfs[i] = fsum[16 * i : 16 * i + 16, :]
    for j in range(4):
        i = order(j)
        peer_send(rfs.at[i], rf.at[zl], rf_ss.at[i], rf_rs.at[zl], i)

    for i in range(4):
        arrived(rkv.at[i], rk_rs.at[i])
        arrived(rq.at[i], rq_rs.at[i])
        arrived(rf.at[i], rf_rs.at[i])

    for n, device in ((0, partner), (1, sibling), (2, sibling)):
        rdma(up.at[0], up.at[0], up_ss.at[n], up_ss.at[n], device).wait_send()
    for i in range(4):
        peer_sent(kvs.at[i, 0:16, :], pk_ss.at[i], i)
        peer_sent(qts.at[i], qt_ss.at[i], i)
        peer_sent(kvs.at[i], kv_ss.at[i], i)
        peer_sent(ots.at[i], ot_ss.at[i], i)
        peer_sent(rks.at[i], rk_ss.at[i], i)
        peer_sent(rqs.at[i], rq_ss.at[i], i)
        peer_sent(rfs.at[i], rf_ss.at[i], i)
        rdma(kvs.at[i], kvs.at[i], fw_ss.at[i], fw_ss.at[i], sibling).wait_send()
        rdma(sse.at[i], sse.at[i], si_ss.at[i], si_ss.at[i], sibling).wait_send()
    for t in range(1, nseg):
        for cc in range(2):
            device = dev(far_seg(t), z, xh, cc)
            rdma(pick, pick, fa_ss.at[t, cc], fa_ss.at[t, cc], device).wait_send()
            rdma(pick, pick, fb_ss.at[t, cc], fb_ss.at[t, cc], device).wait_send()
    rdma(pick, pick, fa_ss.at[0, 0], fa_ss.at[0, 0], sibling).wait_send()
    rdma(pick, pick, fb_ss.at[0, 0], fb_ss.at[0, 0], sibling).wait_send()


def home_kernel(off_ref, rkv, rq, rf, dq_ref, dk_ref, dv_ref, sums):
    ctx = lax.axis_index("context")
    hd = lax.axis_index("heads")
    zl = lax.rem(ctx, 4)
    row = iota((256, 256), 0)
    col = iota((256, 256), 1)
    low_half = iota((256, 128), 1) < 64
    picked = pl.ds(pl.multiple_of(16 * zl, 16), 16)
    for h in range(4):
        sums[h] = rkv[h].astype(F32)
        sums[h, picked, :] = sums[h, picked, :] + rf[h]
    for pair in range(2):
        lanes = slice(128 * pair, 128 * pair + 128)
        both_q = rq[2 * pair : 2 * pair + 2].reshape(128, 256)
        back, queries = [], []
        for h in (2 * pair, 2 * pair + 1):
            perm = (col == place(row, off_ref[hd * 4 + h], zl)).astype(F32).astype(BF)
            back.append(nn(perm, sums[h].astype(BF)))
            queries.append(nt(perm, both_q))
        dq_ref[:, lanes] = jnp.where(low_half, queries[0], queries[1]).astype(BF)
        dk_ref[:, lanes] = jnp.where(low_half, back[0], pltpu.roll(back[1], 64, 1)).astype(BF)
        dv_ref[:, lanes] = jnp.where(low_half, pltpu.roll(back[0], 64, 1), back[1]).astype(BF)


def solution(mesh):
    nseg = mesh.shape["context"] // Z
    vmem = pl.BlockSpec(memory_space=pltpu.VMEM)
    smem = pl.BlockSpec(memory_space=pltpu.SMEM)
    hbm = pl.BlockSpec(memory_space=pltpu.HBM)
    dma = pltpu.SemaphoreType.DMA

    def body(upstream, out_weight, query_rows, key_rows, value_rows, head_offsets):
        width = upstream.shape[1]
        rkv, rq, rf = pl.pallas_call(
            functools.partial(attn_kernel, nseg),
            out_shape=(
                jax.ShapeDtypeStruct((4, 256, 128), BF),
                jax.ShapeDtypeStruct((4, 64, 256), BF),
                jax.ShapeDtypeStruct((4, 16, 128), F32),
            ),
            in_specs=[hbm] * 6,
            out_specs=(vmem, vmem, vmem),
            scratch_shapes=[
                pltpu.SMEM((16,), jnp.int32),
                pltpu.VMEM(out_weight.shape, BF),
                pltpu.VMEM(query_rows.shape, BF),
                pltpu.VMEM(key_rows.shape, BF),
                pltpu.VMEM(value_rows.shape, BF),
                pltpu.VMEM((4, 256, 128), BF),
                pltpu.VMEM((4, 64, 256), BF),
                pltpu.VMEM((4, 64, 256), BF),
                pltpu.VMEM((Z, 256, 128), BF),
                pltpu.VMEM((Z, 64, 256), BF),
                pltpu.VMEM((4, 128, 256), BF),
                pltpu.VMEM((4, 128, 256), BF),
                pltpu.VMEM((4, 64, width), BF),
                pltpu.VMEM((64, 128), BF),
                pltpu.VMEM((nseg, 2, 64, 128), BF),
                pltpu.VMEM((64, nseg * 128), BF),
                pltpu.VMEM((Z, 4, 256, 256), F32),
                pltpu.VMEM((Z, 4, 256, 256), F32),
                pltpu.VMEM((4, 16, 256), F32),
                pltpu.VMEM((4, 16, 256), F32),
                pltpu.VMEM((4, 16, 256), F32),
                pltpu.VMEM((nseg * 128, 128), F32),
                pltpu.VMEM((nseg * 128, 128), F32),
                pltpu.VMEM((4, 64, 256), F32),
                pltpu.VMEM((nseg, 2, 64, 128), BF),
                pltpu.VMEM((nseg, 2, 64, 128), BF),
                pltpu.VMEM((4, 256, 128), BF),
                pltpu.VMEM((4, 256, 128), BF),
                pltpu.VMEM((4, 256, 128), BF),
                pltpu.VMEM((4, 64, 256), BF),
                pltpu.VMEM((4, 16, 128), F32),
                dma((6,)),
                dma((3,)), dma((3,)),
                dma((4,)), dma((4,)),
                dma((4,)), dma((Z,)), dma((4,)),
                dma((4,)), dma((4,)),
                dma((4,)), dma((4,)),
                dma((nseg, 2)), dma((nseg, 2)),
                dma((nseg, 2)), dma((nseg, 2)),
                dma((4,)), dma((4,)),
                dma((4,)), dma((4,)),
                dma((4,)), dma((4,)),
                dma((4,)), dma((4,)),
            ],
            compiler_params=pltpu.CompilerParams(
                collective_id=0, has_side_effects=True, vmem_limit_bytes=66400000
            ),
            name="attn",
        )(head_offsets, upstream, out_weight, query_rows, key_rows, value_rows)
        block = jax.ShapeDtypeStruct(query_rows.shape, BF)
        return pl.pallas_call(
            home_kernel,
            out_shape=(block, block, block),
            in_specs=[smem, vmem, vmem, vmem],
            out_specs=(vmem, vmem, vmem),
            scratch_shapes=[pltpu.VMEM((4, 256, 128), F32)],
            name="home",
        )(head_offsets, rkv, rq, rf)

    return jax.shard_map(
        body,
        mesh=mesh,
        in_specs=(
            P(("context", "heads"), None),
            P("heads", None),
            P("context", "heads"),
            P("context", "heads"),
            P("context", "heads"),
            P(),
        ),
        out_specs=(P("context", "heads"), P("context", "heads"), P("context", "heads")),
        check_vma=False,
    )
```

time: 56.9 us -> 48 us (0.84)
  local copies, waits for them, and re-layouts: 6.63 us -> 0 us
  Pallas kernels: 49.3 us -> 47.2 us
    unnamed x16 -> x0, local copies, waits for them, and re-layouts: 6.63 us -> none
    pallas_call x1, Pallas kernels: 47.2 us -> 45 us  [body(): pl.pallas_call(functools.partial(attn_kernel, nseg), out_shape=(jax.Shape...]
where the time goes in v2:
time: 48 us; the launch traced here: 47.9 us
  Pallas kernels  47.2 us (98%)
  between operations  0.64 us (1%)
    pallas_call x1, Pallas kernels, body(): pl.pallas_call(functools.partial(attn_kernel, nseg), out_shape=(jax.Shape...  45 us
    pallas_call x1, Pallas kernels, body(): pl.pallas_call(home_kernel, out_shape=(block, block, block), in_specs=[sm...  2.25 us

profile of v2, /device:TPU:1, one launch (start us, length us, event | category | flops | bytes accessed | tf_op | source)
XLA Modules:
  0.0 47.9 jit_solution(7181903705209868645)
XLA Ops:
  0.6 45.0 %attn.1 = (bf16[4,256,128]{2,1,0:T(8,128)(2,1)}, bf16[4,64,256]{2,1,0:T(8,128)(2,1)}, f32[4,16,128]{2,1,0:T(8,128)}) custom-call(s32[16]{0:T(128)} %off_ref.1, bf16[64,1024]{1,0:T(8,128)(2,1)} %up_h.1, bf16[256,1024]{1,0:T(8,128)(2,1)} %w_h.1, bf16[256,256]{1,0:T(8,128)(2,1)} %q_h.1, bf16[256,256]{1,0:T(8,128)(2,1)} %k_h.1, bf16[256,256]{1,0:T(8,128)(2,1)} %v_h.1), custom_call_target="tpu_custom_call" | custom-call | tf_op jit(solution)/shard_map/attn/pallas_call | solution.py:390
  45.6 2.3 %home.1 = (bf16[256,256]{1,0:T(8,128)(2,1)}, bf16[256,256]{1,0:T(8,128)(2,1)}, bf16[256,256]{1,0:T(8,128)(2,1)}) custom-call(s32[16]{0:T(128)} %off_ref.1, bf16[4,256,128]{2,1,0:T(8,128)(2,1)} %get-tuple-element.6.rkv, bf16[4,64,256]{2,1,0:T(8,128)(2,1)} %get-tuple-element.7.rq, f32[4,16,128]{2,1,0:T(8,128)} %get-tuple-element.8.rf), custom_call_target="tpu_custom_call" | custom-call | tf_op jit(solution)/shard_map/home/pallas_call | solution.py:450

commit v3 on v2

--- a/solution.py
+++ b/solution.py
@@ -29,6 +29,10 @@
 
 def place(rows, offset, zl):
     return 16 * (((rows & 15) - offset + zl + 16) & 15) + (rows >> 4)
+
+
+def origin(places, offset, zl):
+    return 16 * (places & 15) + (((places >> 4) + offset - zl + 16) & 15)
 
 
 def attn_kernel(
@@ -122,7 +126,7 @@
         ot[b, 0:64, :] = jnp.zeros((64, 256), BF)
     m_s[...] = jnp.full(m_s.shape, LOW, F32)
     l_s[...] = jnp.zeros(l_s.shape, F32)
-    row = iota((256, 256), 1)
+    row = iota((1, 256), 1)
     col = iota((256, 256), 0)
     low_half = iota((256, 128), 1) < 64
     lane = iota((1, 128), 1)
@@ -130,14 +134,17 @@
     for load in loads[:4]:
         load.wait()
     q_t = q_ref[...].astype(F32).T.astype(BF)
+    k_v = [
+        jnp.concatenate([k_ref[:, n : n + 128], v_ref[:, n : n + 128]], axis=1) for n in (0, 128)
+    ]
     perms = []
     for h in range(4):
         perm = (col == place(row, off_ref[hd * 4 + h], zl)).astype(F32).astype(BF)
         perms.append(perm)
         qts[h] = (nt(q_t[64 * h : 64 * h + 64, :], perm) * 0.125).astype(BF)
-        lanes = slice(128 * (h // 2), 128 * (h // 2) + 128)
-        k_p = nn(perm, k_ref[:, lanes])
-        v_p = nn(perm, v_ref[:, lanes])
+        both = nn(perm, k_v[h // 2])
+        k_p = both[:, 0:128]
+        v_p = both[:, 128:256]
         if h % 2:
             k_p = pltpu.roll(k_p, 64, 1)
         else:
@@ -289,14 +296,16 @@
         acc_s[b, :, 128:256] = jnp.zeros((64, 128), F32)
 
     def grad_block(d):
-        grads = jnp.zeros((256, 128), F32)
+        key_grads = jnp.zeros((64, 256), F32)
+        value_grads = jnp.zeros((64, 256), F32)
         keys_t = kt[d]
         for b in range(4):
             p = ex[d, b] * f_s[b, pl.ds(d, 1), :]
             ds = (p * (dp[d, b] - l_s[b, 0:1, :])).astype(BF)
-            grads = grads + nt(ds, qt[b]) + nt(p.astype(BF), ot[b])
+            key_grads = key_grads + nt(qt[b, 0:64, :], ds)
+            value_grads = value_grads + nt(ot[b, 64:128, :], p.astype(BF))
             acc_s[b] = acc_s[b] + nn(keys_t, ds)
-        return grads
+        return jnp.concatenate([key_grads, value_grads], axis=0)
 
     def pair_block(n, carry):
         i = lax.rem(zl + n, 4)
@@ -328,11 +337,6 @@
         i = order(j)
         peer_send(rfs.at[i], rf.at[zl], rf_ss.at[i], rf_rs.at[zl], i)
 
-    for i in range(4):
-        arrived(rkv.at[i], rk_rs.at[i])
-        arrived(rq.at[i], rq_rs.at[i])
-        arrived(rf.at[i], rf_rs.at[i])
-
     for n, device in ((0, partner), (1, sibling), (2, sibling)):
         rdma(up.at[0], up.at[0], up_ss.at[n], up_ss.at[n], device).wait_send()
     for i in range(4):
@@ -353,25 +357,35 @@
     rdma(pick, pick, fa_ss.at[0, 0], fa_ss.at[0, 0], sibling).wait_send()
     rdma(pick, pick, fb_ss.at[0, 0], fb_ss.at[0, 0], sibling).wait_send()
 
-
-def home_kernel(off_ref, rkv, rq, rf, dq_ref, dk_ref, dv_ref, sums):
+    for i in range(4):
+        arrived(rkv.at[i], rk_rs.at[i])
+        arrived(rq.at[i], rq_rs.at[i])
+        arrived(rf.at[i], rf_rs.at[i])
+
+
+def home_kernel(off_ref, rkv, rq, rf, dq_ref, dk_ref, dv_ref):
     ctx = lax.axis_index("context")
     hd = lax.axis_index("heads")
     zl = lax.rem(ctx, 4)
     row = iota((256, 256), 0)
-    col = iota((256, 256), 1)
+    col = iota((1, 256), 1)
     low_half = iota((256, 128), 1) < 64
-    picked = pl.ds(pl.multiple_of(16 * zl, 16), 16)
-    for h in range(4):
-        sums[h] = rkv[h].astype(F32)
-        sums[h, picked, :] = sums[h, picked, :] + rf[h]
+    pick = iota((1, 128), 1)
+    pick_row = iota((256, 128), 0)
     for pair in range(2):
         lanes = slice(128 * pair, 128 * pair + 128)
         both_q = rq[2 * pair : 2 * pair + 2].reshape(128, 256)
         back, queries = [], []
         for h in (2 * pair, 2 * pair + 1):
-            perm = (col == place(row, off_ref[hd * 4 + h], zl)).astype(F32).astype(BF)
-            back.append(nn(perm, sums[h].astype(BF)))
+            perm = (row == origin(col, off_ref[hd * 4 + h], zl)).astype(F32).astype(BF)
+            back_pick = jnp.logical_and(
+                pick < 16, pick_row == origin(16 * zl + (pick & 15), off_ref[hd * 4 + h], zl)
+            )
+            far = jnp.concatenate([rf[h], jnp.zeros((112, 128), F32)], axis=0)
+            high = far.astype(BF)
+            low = (far - high.astype(F32)).astype(BF)
+            back_pick = back_pick.astype(F32).astype(BF)
+            back.append(nt(perm, rkv[h]) + nn(back_pick, high) + nn(back_pick, low))
             queries.append(nt(perm, both_q))
         dq_ref[:, lanes] = jnp.where(low_half, queries[0], queries[1]).astype(BF)
         dk_ref[:, lanes] = jnp.where(low_half, back[0], pltpu.roll(back[1], 64, 1)).astype(BF)
@@ -390,12 +404,12 @@
         rkv, rq, rf = pl.pallas_call(
             functools.partial(attn_kernel, nseg),
             out_shape=(
-                jax.ShapeDtypeStruct((4, 256, 128), BF),
+                jax.ShapeDtypeStruct((4, 128, 256), BF),
                 jax.ShapeDtypeStruct((4, 64, 256), BF),
                 jax.ShapeDtypeStruct((4, 16, 128), F32),
             ),
             in_specs=[hbm] * 6,
-            out_specs=(vmem, vmem, vmem),
+            out_specs=(hbm, hbm, hbm),
             scratch_shapes=[
                 pltpu.SMEM((16,), jnp.int32),
                 pltpu.VMEM(out_weight.shape, BF),
@@ -423,9 +437,9 @@
                 pltpu.VMEM((4, 64, 256), F32),
                 pltpu.VMEM((nseg, 2, 64, 128), BF),
                 pltpu.VMEM((nseg, 2, 64, 128), BF),
-                pltpu.VMEM((4, 256, 128), BF),
-                pltpu.VMEM((4, 256, 128), BF),
-                pltpu.VMEM((4, 256, 128), BF),
+                pltpu.VMEM((4, 128, 256), BF),
+                pltpu.VMEM((4, 128, 256), BF),
+                pltpu.VMEM((4, 128, 256), BF),
                 pltpu.VMEM((4, 64, 256), BF),
                 pltpu.VMEM((4, 16, 128), F32),
                 dma((6,)),
@@ -452,7 +466,6 @@
             out_shape=(block, block, block),
             in_specs=[smem, vmem, vmem, vmem],
             out_specs=(vmem, vmem, vmem),
-            scratch_shapes=[pltpu.VMEM((4, 256, 128), F32)],
             name="home",
         )(head_offsets, rkv, rq, rf)
 

time: 48 us -> 46.8 us (0.975)
  Pallas kernels: 47.2 us -> 46 us
    pallas_call x1, Pallas kernels: 45 us -> 43.6 us  [body(): pl.pallas_call(functools.partial(attn_kernel, nseg), out_shape=(jax.Shape...]
where the time goes in v3:
time: 46.8 us; the launch traced here: 46.6 us
  Pallas kernels  46 us (98%)
  between operations  0.64 us (1%)
    pallas_call x1, Pallas kernels, body(): pl.pallas_call(functools.partial(attn_kernel, nseg), out_shape=(jax.Shape...  43.6 us
    pallas_call x1, Pallas kernels, body(): pl.pallas_call(home_kernel, out_shape=(block, block, block), in_specs=[sm...  2.37 us

profile of v3, /device:TPU:1, one launch (start us, length us, event | category | flops | bytes accessed | tf_op | source)
XLA Modules:
  0.0 46.6 jit_solution(1064496562392714144)
XLA Ops:
  0.6 43.6 %attn.1 = (bf16[4,128,256]{2,1,0:T(8,128)(2,1)}, bf16[4,64,256]{2,1,0:T(8,128)(2,1)}, f32[4,16,128]{2,1,0:T(8,128)}) custom-call(s32[16]{0:T(128)} %off_ref.1, bf16[64,1024]{1,0:T(8,128)(2,1)} %up_h.1, bf16[256,1024]{1,0:T(8,128)(2,1)} %w_h.1, bf16[256,256]{1,0:T(8,128)(2,1)} %q_h.1, bf16[256,256]{1,0:T(8,128)(2,1)} %k_h.1, bf16[256,256]{1,0:T(8,128)(2,1)} %v_h.1), custom_call_target="tpu_custom_call" | custom-call | tf_op jit(solution)/shard_map/attn/pallas_call | solution.py:404
  44.3 2.4 %home.1 = (bf16[256,256]{1,0:T(8,128)(2,1)}, bf16[256,256]{1,0:T(8,128)(2,1)}, bf16[256,256]{1,0:T(8,128)(2,1)}) custom-call(s32[16]{0:T(128)} %off_ref.1, bf16[4,128,256]{2,1,0:T(8,128)(2,1)} %get-tuple-element.6.rkv, bf16[4,64,256]{2,1,0:T(8,128)(2,1)} %get-tuple-element.7.rq, f32[4,16,128]{2,1,0:T(8,128)} %get-tuple-element.8.rf), custom_call_target="tpu_custom_call" | custom-call | tf_op jit(solution)/shard_map/home/pallas_call | solution.py:464

commit v4 on v3

--- a/solution.py
+++ b/solution.py
@@ -94,8 +94,20 @@
     def arrived(dst, rs):
         pltpu.make_async_copy(dst, dst, rs).wait()
 
+    code = jnp.where(zl < 2, jnp.where(zl == 0, 228, 225), jnp.where(zl == 2, 54, 27))
+    near_last = [lax.rem(lax.div(code, 4**j), 4) for j in range(4)]
+
+    def order_of(half, j):
+        return jnp.where(half == zh, near_last[3 - j], near_last[j])
+
     def order(j):
-        return lax.rem(zl + j, 4)
+        return order_of(c, j)
+
+    def step_of(half, j):
+        out = order_of(half, 3)
+        for n in range(3):
+            out = jnp.where(j == n, order_of(half, n), out)
+        return out
 
     bar = pltpu.get_barrier_semaphore()
 
@@ -205,7 +217,7 @@
             l_s[b, pl.ds(d, 1), :] = jnp.sum(e, axis=0, keepdims=True)
 
     def own_block(j, carry):
-        i = lax.rem(zl + 4 - j, 4)
+        i = step_of(c, j)
         d = 4 * c + i
         arrived(kv.at[d], kv_rs.at[d])
         rdma(kv.at[d], kv.at[d], fw_ss.at[i], kv_rs.at[d], sibling).start()
@@ -213,7 +225,7 @@
         return carry
 
     def other_block(j, carry):
-        d = 4 * oc + lax.rem(zl + 4 - j, 4)
+        d = 4 * oc + step_of(oc, j)
         arrived(kv.at[d], kv_rs.at[d])
         score_block(d)
         return carry
@@ -252,48 +264,36 @@
         f_s[b] = jnp.exp(m_all - lse)
     fe[...] = fe[...] * gather_lanes([f_s[b, Z : Z + 1, 0:128] for b in range(4)])
 
-    for b in range(4):
+    for j in range(4):
+        b = order(j)
         arrived(ot.at[b, 64:128, :], ot_rs.at[b])
+        o_b = ot[b]
+
+        def dprob_blocks(n, total):
+            for m in range(4):
+                d = 4 * n + m
+                g = nn(kv[d], o_b)
+                dp[d, b] = g
+                part = jnp.sum(ex[d, b] * g, axis=0, keepdims=True)
+                total = total + f_s[b, pl.ds(d, 1), :] * part
+            return total
+
+        l_s[b, 0:1, :] = lax.fori_loop(0, 2, dprob_blocks, jnp.zeros((1, 256), F32))
+
     o_far = gather_lanes([ot[b, :, 0:128].astype(F32) for b in range(4)]).astype(BF)
     g_far = nn(fk[...].reshape(nseg * 128, 128), o_far)
     fds[...] = g_far
     far_delta = jnp.sum(fe[...] * g_far, axis=0, keepdims=True)
-
-    def dprob_block(d, total):
-        keys = kv[d]
-        out = []
-        for b in range(4):
-            g = nn(keys, ot[b])
-            dp[d, b] = g
-            part = jnp.sum(ex[d, b] * g, axis=0, keepdims=True)
-            out.append(total[b] + f_s[b, pl.ds(d, 1), :] * part)
-        return tuple(out)
-
-    delta = lax.fori_loop(0, Z, dprob_block, tuple(jnp.zeros((1, 256), F32) for _ in range(4)))
     zero_row = jnp.zeros((1, 128), F32)
     delta = [
-        delta[b] + jnp.concatenate([jnp.where(mine(b), far_delta, 0.0), zero_row], axis=1)
+        l_s[b, 0:1, :] + jnp.concatenate([jnp.where(mine(b), far_delta, 0.0), zero_row], axis=1)
         for b in range(4)
     ]
     for b in range(4):
         l_s[b, 0:1, :] = delta[b]
 
-    p_far = fe[...]
-    ds_far = (p_far * (fds[...] - gather_lanes([delta[b][:, 0:128] for b in range(4)]))).astype(BF)
-    dkv_far = nt(ds_far, q_far) + nt(p_far.astype(BF), o_far)
-    fse[...] = dkv_far.astype(BF).reshape(nseg, 2, 64, 128)
-    for t in range(1, nseg):
-        for cc in range(2):
-            rdma(
-                fse.at[far_seg(t), cc], fre.at[s, c], fb_ss.at[t, cc], fb_rs.at[s, c],
-                dev(far_seg(t), z, xh, cc),
-            ).start()
-    rdma(fse.at[s, oc], fre.at[s, c], fb_ss.at[0, 0], fb_rs.at[s, c], sibling).start()
-    fre[s, c] = fse[s, c]
-    dq_far = nn(fkt[...], ds_far)
     for b in range(4):
-        acc_s[b, :, 0:128] = jnp.where(mine(b), dq_far, 0.0)
-        acc_s[b, :, 128:256] = jnp.zeros((64, 128), F32)
+        acc_s[b] = jnp.zeros((64, 256), F32)
 
     def grad_block(d):
         key_grads = jnp.zeros((64, 256), F32)
@@ -308,16 +308,35 @@
         return jnp.concatenate([key_grads, value_grads], axis=0)
 
     def pair_block(n, carry):
-        i = lax.rem(zl + n, 4)
+        i = step_of(oc, n)
         sse[i] = grad_block(4 * oc + i).astype(BF)
         rdma(sse.at[i], sre.at[i], si_ss.at[i], si_rs.at[i], sibling).start()
+        i = step_of(c, n)
         grads = grad_block(4 * c + i)
         arrived(sre.at[i], si_rs.at[i])
         rks[i] = (grads + sre[i].astype(F32)).astype(BF)
         peer_send(rks.at[i], rkv.at[zl], rk_ss.at[i], rk_rs.at[zl], i)
         return carry
 
-    lax.fori_loop(0, 4, pair_block, 0)
+    lax.fori_loop(0, 1, pair_block, 0)
+
+    p_far = fe[...]
+    ds_far = (p_far * (fds[...] - gather_lanes([delta[b][:, 0:128] for b in range(4)]))).astype(BF)
+    dkv_far = nt(ds_far, q_far) + nt(p_far.astype(BF), o_far)
+    fse[...] = dkv_far.astype(BF).reshape(nseg, 2, 64, 128)
+    for t in range(1, nseg):
+        for cc in range(2):
+            rdma(
+                fse.at[far_seg(t), cc], fre.at[s, c], fb_ss.at[t, cc], fb_rs.at[s, c],
+                dev(far_seg(t), z, xh, cc),
+            ).start()
+    rdma(fse.at[s, oc], fre.at[s, c], fb_ss.at[0, 0], fb_rs.at[s, c], sibling).start()
+    fre[s, c] = fse[s, c]
+    dq_far = nn(fkt[...], ds_far)
+    for b in range(4):
+        acc_s[b, :, 0:128] = acc_s[b, :, 0:128] + jnp.where(mine(b), dq_far, 0.0)
+
+    lax.fori_loop(1, 4, pair_block, 0)
     for j in range(4):
         b = order(j)
         rqs[b] = (acc_s[b] * 0.125).astype(BF)

time: 46.8 us -> 46.5 us (level)
  no operation moved by 1% of the time
where the time goes in v4:
time: 46.5 us; the launch traced here: 46.4 us
  Pallas kernels  45.7 us (98%)
  between operations  0.64 us (1%)
    pallas_call x1, Pallas kernels, body(): pl.pallas_call(functools.partial(attn_kernel, nseg), out_shape=(jax.Shape...  43.4 us
    pallas_call x1, Pallas kernels, body(): pl.pallas_call(home_kernel, out_shape=(block, block, block), in_specs=[sm...  2.38 us

profile of v4, /device:TPU:1, one launch (start us, length us, event | category | flops | bytes accessed | tf_op | source)
XLA Modules:
  0.0 46.4 jit_solution(12587797056205513545)
XLA Ops:
  0.6 43.4 %attn.1 = (bf16[4,128,256]{2,1,0:T(8,128)(2,1)}, bf16[4,64,256]{2,1,0:T(8,128)(2,1)}, f32[4,16,128]{2,1,0:T(8,128)}) custom-call(s32[16]{0:T(128)} %off_ref.1, bf16[64,1024]{1,0:T(8,128)(2,1)} %up_h.1, bf16[256,1024]{1,0:T(8,128)(2,1)} %w_h.1, bf16[256,256]{1,0:T(8,128)(2,1)} %q_h.1, bf16[256,256]{1,0:T(8,128)(2,1)} %k_h.1, bf16[256,256]{1,0:T(8,128)(2,1)} %v_h.1), custom_call_target="tpu_custom_call" | custom-call | tf_op jit(solution)/shard_map/attn/pallas_call | solution.py:423
  44.0 2.4 %home.1 = (bf16[256,256]{1,0:T(8,128)(2,1)}, bf16[256,256]{1,0:T(8,128)(2,1)}, bf16[256,256]{1,0:T(8,128)(2,1)}) custom-call(s32[16]{0:T(128)} %off_ref.1, bf16[4,128,256]{2,1,0:T(8,128)(2,1)} %get-tuple-element.6.rkv, bf16[4,64,256]{2,1,0:T(8,128)(2,1)} %get-tuple-element.7.rq, f32[4,16,128]{2,1,0:T(8,128)} %get-tuple-element.8.rf), custom_call_target="tpu_custom_call" | custom-call | tf_op jit(solution)/shard_map/home/pallas_call | solution.py:483

commit v5 on v4

--- a/solution.py
+++ b/solution.py
@@ -143,18 +143,31 @@
     low_half = iota((256, 128), 1) < 64
     lane = iota((1, 128), 1)
 
-    for load in loads[:4]:
+    for load in loads[:2]:
         load.wait()
     q_t = q_ref[...].astype(F32).T.astype(BF)
-    k_v = [
-        jnp.concatenate([k_ref[:, n : n + 128], v_ref[:, n : n + 128]], axis=1) for n in (0, 128)
-    ]
     perms = []
     for h in range(4):
         perm = (col == place(row, off_ref[hd * 4 + h], zl)).astype(F32).astype(BF)
         perms.append(perm)
         qts[h] = (nt(q_t[64 * h : 64 * h + 64, :], perm) * 0.125).astype(BF)
-        both = nn(perm, k_v[h // 2])
+    loads[4].wait()
+
+    pl.semaphore_wait(bar, 4 + 2 + 2 * (nseg - 1) - jnp.where(zh == c, 1, 0))
+
+    rdma(up.at[hd], up.at[hd], up_ss.at[0], up_rs.at[0], partner).start()
+    rdma(up.at[hd], up.at[hd], up_ss.at[1], up_rs.at[1], sibling).start()
+    for j in range(4):
+        i = order(j)
+        peer_send(qts.at[i], qt.at[zl, 0:64, :], qt_ss.at[i], qt_rs.at[zl], i)
+
+    for load in loads[2:4]:
+        load.wait()
+    k_v = [
+        jnp.concatenate([k_ref[:, n : n + 128], v_ref[:, n : n + 128]], axis=1) for n in (0, 128)
+    ]
+    for h in range(4):
+        both = nn(perms[h], k_v[h // 2])
         k_p = both[:, 0:128]
         v_p = both[:, 128:256]
         if h % 2:
@@ -162,19 +175,10 @@
         else:
             v_p = pltpu.roll(v_p, 64, 1)
         kvs[h] = jnp.where(low_half, k_p, v_p).astype(BF)
-    loads[4].wait()
-
-    pl.semaphore_wait(bar, 4 + 2 + 2 * (nseg - 1) - jnp.where(zh == c, 1, 0))
-
     picked = pl.ds(pl.multiple_of(16 * zl, 16), 16)
-    rdma(up.at[hd], up.at[hd], up_ss.at[0], up_rs.at[0], partner).start()
-    rdma(up.at[hd], up.at[hd], up_ss.at[1], up_rs.at[1], sibling).start()
     for j in range(4):
         i = order(j)
         peer_send(kvs.at[i, picked, :], pick.at[picked, :], pk_ss.at[i], pk_rs.at[zl], i)
-    for j in range(4):
-        i = order(j)
-        peer_send(qts.at[i], qt.at[zl, 0:64, :], qt_ss.at[i], qt_rs.at[zl], i)
     for j in range(4):
         i = order(j)
         peer_send(kvs.at[i], kv.at[z], kv_ss.at[i], kv_rs.at[z], i)

time: 46.5 us -> 46.1 us (level)
  no operation moved by 1% of the time
where the time goes in v5:
time: 46.1 us; the launch traced here: 46 us
  Pallas kernels  45.4 us (98%)
  between operations  0.64 us (1%)
    pallas_call x1, Pallas kernels, body(): pl.pallas_call(functools.partial(attn_kernel, nseg), out_shape=(jax.Shape...  43 us
    pallas_call x1, Pallas kernels, body(): pl.pallas_call(home_kernel, out_shape=(block, block, block), in_specs=[sm...  2.37 us

profile of v5, /device:TPU:1, one launch (start us, length us, event | category | flops | bytes accessed | tf_op | source)
XLA Modules:
  0.0 46.0 jit_solution(8050552738871254777)
XLA Ops:
  0.6 43.0 %attn.1 = (bf16[4,128,256]{2,1,0:T(8,128)(2,1)}, bf16[4,64,256]{2,1,0:T(8,128)(2,1)}, f32[4,16,128]{2,1,0:T(8,128)}) custom-call(s32[16]{0:T(128)} %off_ref.1, bf16[64,1024]{1,0:T(8,128)(2,1)} %up_h.1, bf16[256,1024]{1,0:T(8,128)(2,1)} %w_h.1, bf16[256,256]{1,0:T(8,128)(2,1)} %q_h.1, bf16[256,256]{1,0:T(8,128)(2,1)} %k_h.1, bf16[256,256]{1,0:T(8,128)(2,1)} %v_h.1), custom_call_target="tpu_custom_call" | custom-call | tf_op jit(solution)/shard_map/attn/pallas_call | solution.py:427
  43.7 2.4 %home.1 = (bf16[256,256]{1,0:T(8,128)(2,1)}, bf16[256,256]{1,0:T(8,128)(2,1)}, bf16[256,256]{1,0:T(8,128)(2,1)}) custom-call(s32[16]{0:T(128)} %off_ref.1, bf16[4,128,256]{2,1,0:T(8,128)(2,1)} %get-tuple-element.6.rkv, bf16[4,64,256]{2,1,0:T(8,128)(2,1)} %get-tuple-element.7.rq, f32[4,16,128]{2,1,0:T(8,128)} %get-tuple-element.8.rf), custom_call_target="tpu_custom_call" | custom-call | tf_op jit(solution)/shard_map/home/pallas_call | solution.py:487

commit v6 on v5

--- a/solution.py
+++ b/solution.py
@@ -311,18 +311,24 @@
             acc_s[b] = acc_s[b] + nn(keys_t, ds)
         return jnp.concatenate([key_grads, value_grads], axis=0)
 
-    def pair_block(n, carry):
+    def sibling_block(n):
         i = step_of(oc, n)
         sse[i] = grad_block(4 * oc + i).astype(BF)
         rdma(sse.at[i], sre.at[i], si_ss.at[i], si_rs.at[i], sibling).start()
+
+    def own_grads(n):
         i = step_of(c, n)
         grads = grad_block(4 * c + i)
         arrived(sre.at[i], si_rs.at[i])
         rks[i] = (grads + sre[i].astype(F32)).astype(BF)
         peer_send(rks.at[i], rkv.at[zl], rk_ss.at[i], rk_rs.at[zl], i)
+
+    def pair_block(n, carry):
+        sibling_block(n + 1)
+        own_grads(n)
         return carry
 
-    lax.fori_loop(0, 1, pair_block, 0)
+    sibling_block(0)
 
     p_far = fe[...]
     ds_far = (p_far * (fds[...] - gather_lanes([delta[b][:, 0:128] for b in range(4)]))).astype(BF)
@@ -340,7 +346,8 @@
     for b in range(4):
         acc_s[b, :, 0:128] = acc_s[b, :, 0:128] + jnp.where(mine(b), dq_far, 0.0)
 
-    lax.fori_loop(1, 4, pair_block, 0)
+    lax.fori_loop(0, 3, pair_block, 0)
+    own_grads(3)
     for j in range(4):
         b = order(j)
         rqs[b] = (acc_s[b] * 0.125).astype(BF)
@@ -402,13 +409,13 @@
         for h in (2 * pair, 2 * pair + 1):
             perm = (row == origin(col, off_ref[hd * 4 + h], zl)).astype(F32).astype(BF)
             back_pick = jnp.logical_and(
-                pick < 16, pick_row == origin(16 * zl + (pick & 15), off_ref[hd * 4 + h], zl)
+                pick < 32, pick_row == origin(16 * zl + (pick & 15), off_ref[hd * 4 + h], zl)
             )
-            far = jnp.concatenate([rf[h], jnp.zeros((112, 128), F32)], axis=0)
-            high = far.astype(BF)
-            low = (far - high.astype(F32)).astype(BF)
+            high = rf[h].astype(BF)
+            low = (rf[h] - high.astype(F32)).astype(BF)
+            far = jnp.concatenate([high, low, jnp.zeros((96, 128), BF)], axis=0)
             back_pick = back_pick.astype(F32).astype(BF)
-            back.append(nt(perm, rkv[h]) + nn(back_pick, high) + nn(back_pick, low))
+            back.append(nt(perm, rkv[h]) + nn(back_pick, far))
             queries.append(nt(perm, both_q))
         dq_ref[:, lanes] = jnp.where(low_half, queries[0], queries[1]).astype(BF)
         dk_ref[:, lanes] = jnp.where(low_half, back[0], pltpu.roll(back[1], 64, 1)).astype(BF)

time: 46.1 us -> 45.3 us (0.983)
  Pallas kernels: 45.4 us -> 44.5 us
    pallas_call x1, Pallas kernels: 43 us -> 42.2 us  [body(): pl.pallas_call(functools.partial(attn_kernel, nseg), out_shape=(jax.Shape...]
where the time goes in v6:
time: 45.3 us; the launch traced here: 45.2 us
  Pallas kernels  44.5 us (98%)
  between operations  0.64 us (1%)
    pallas_call x1, Pallas kernels, body(): pl.pallas_call(functools.partial(attn_kernel, nseg), out_shape=(jax.Shape...  42.2 us
    pallas_call x1, Pallas kernels, body(): pl.pallas_call(home_kernel, out_shape=(block, block, block), in_specs=[sm...  2.32 us

profile of v6, /device:TPU:1, one launch (start us, length us, event | category | flops | bytes accessed | tf_op | source)
XLA Modules:
  0.0 45.2 jit_solution(3581921242175417046)
XLA Ops:
  0.6 42.2 %attn.1 = (bf16[4,128,256]{2,1,0:T(8,128)(2,1)}, bf16[4,64,256]{2,1,0:T(8,128)(2,1)}, f32[4,16,128]{2,1,0:T(8,128)}) custom-call(s32[16]{0:T(128)} %off_ref.1, bf16[64,1024]{1,0:T(8,128)(2,1)} %up_h.1, bf16[256,1024]{1,0:T(8,128)(2,1)} %w_h.1, bf16[256,256]{1,0:T(8,128)(2,1)} %q_h.1, bf16[256,256]{1,0:T(8,128)(2,1)} %k_h.1, bf16[256,256]{1,0:T(8,128)(2,1)} %v_h.1), custom_call_target="tpu_custom_call" | custom-call | tf_op jit(solution)/shard_map/attn/pallas_call | solution.py:434
  42.8 2.3 %home.1 = (bf16[256,256]{1,0:T(8,128)(2,1)}, bf16[256,256]{1,0:T(8,128)(2,1)}, bf16[256,256]{1,0:T(8,128)(2,1)}) custom-call(s32[16]{0:T(128)} %off_ref.1, bf16[4,128,256]{2,1,0:T(8,128)(2,1)} %get-tuple-element.6.rkv, bf16[4,64,256]{2,1,0:T(8,128)(2,1)} %get-tuple-element.7.rq, f32[4,16,128]{2,1,0:T(8,128)} %get-tuple-element.8.rf), custom_call_target="tpu_custom_call" | custom-call | tf_op jit(solution)/shard_map/home/pallas_call | solution.py:494

commit v7 on v6

--- a/solution.py
+++ b/solution.py
@@ -346,7 +346,9 @@
     for b in range(4):
         acc_s[b, :, 0:128] = acc_s[b, :, 0:128] + jnp.where(mine(b), dq_far, 0.0)
 
-    lax.fori_loop(0, 3, pair_block, 0)
+    own_grads(0)
+    sibling_block(1)
+    lax.fori_loop(1, 3, pair_block, 0)
     own_grads(3)
     for j in range(4):
         b = order(j)

time: 45.3 us -> 45.8 us (1.011)
  Pallas kernels: 44.5 us -> 45.1 us
    pallas_call x1, Pallas kernels: 42.2 us -> 42.8 us  [body(): pl.pallas_call(functools.partial(attn_kernel, nseg), out_shape=(jax.Shape...]
where the time goes in v7:
time: 45.8 us; the launch traced here: 45.7 us
  Pallas kernels  45.1 us (98%)
  between operations  0.64 us (1%)
    pallas_call x1, Pallas kernels, body(): pl.pallas_call(functools.partial(attn_kernel, nseg), out_shape=(jax.Shape...  42.8 us
    pallas_call x1, Pallas kernels, body(): pl.pallas_call(home_kernel, out_shape=(block, block, block), in_specs=[sm...  2.31 us

profile of v7, /device:TPU:1, one launch (start us, length us, event | category | flops | bytes accessed | tf_op | source)
XLA Modules:
  0.0 45.7 jit_solution(5398568998204528113)
XLA Ops:
  0.6 42.8 %attn.1 = (bf16[4,128,256]{2,1,0:T(8,128)(2,1)}, bf16[4,64,256]{2,1,0:T(8,128)(2,1)}, f32[4,16,128]{2,1,0:T(8,128)}) custom-call(s32[16]{0:T(128)} %off_ref.1, bf16[64,1024]{1,0:T(8,128)(2,1)} %up_h.1, bf16[256,1024]{1,0:T(8,128)(2,1)} %w_h.1, bf16[256,256]{1,0:T(8,128)(2,1)} %q_h.1, bf16[256,256]{1,0:T(8,128)(2,1)} %k_h.1, bf16[256,256]{1,0:T(8,128)(2,1)} %v_h.1), custom_call_target="tpu_custom_call" | custom-call | tf_op jit(solution)/shard_map/attn/pallas_call | solution.py:436
  43.4 2.3 %home.1 = (bf16[256,256]{1,0:T(8,128)(2,1)}, bf16[256,256]{1,0:T(8,128)(2,1)}, bf16[256,256]{1,0:T(8,128)(2,1)}) custom-call(s32[16]{0:T(128)} %off_ref.1, bf16[4,128,256]{2,1,0:T(8,128)(2,1)} %get-tuple-element.6.rkv, bf16[4,64,256]{2,1,0:T(8,128)(2,1)} %get-tuple-element.7.rq, f32[4,16,128]{2,1,0:T(8,128)} %get-tuple-element.8.rf), custom_call_target="tpu_custom_call" | custom-call | tf_op jit(solution)/shard_map/home/pallas_call | solution.py:496
